TPU v7x, 128 devices: a whole 4x4x4 slice. The times are simulated.
128 devices in a mesh: row: 8 (over y, x_hi), col: 16 (over x_lo, z, core).
Axes of the slice: x: 4 (x_hi: 2, x_lo: 2; x = x_hi * 2 + x_lo), y: 4, z: 4, core: 2. Of those that a mesh axis runs over, the one named last changes fastest.
Arguments:
- local_ops: bfloat16 [8, 16, 2048, 2048], P('row', 'col'), may hold values from -2 to 30, as said below
- loads: float32 [8, 16, 2048, 256], P('row', 'col'), may hold values from -6 to 6
- modes: float32 [8, 16, 32, 2048], P('row', 'col'), may hold values from -1 to 1
- coarse_inverse: float32 [4096, 4096], P('row', 'col'), may hold values from -1 to 1
- face_rows: int32 [8, 16, 4, 512], P('row', 'col'), may hold values from 0 to 2047, as said below
- adjacency: int32 [8, 16, 4], P('row', 'col'), may hold values from 0 to 1, as said below
- contact: int32 [8, 16, 2048], P('row', 'col'), may hold values 0 or 1
Outputs:
- multipliers: float32 [8, 16, 2048, 256], P('row', 'col')
Inputs may be any that keep to these rules, and one draw needn't show every extreme that they name: `face_rows`: for each subdomain the 2048 entries are a permutation of 0 to 2047. `adjacency`: symmetric across each shared face (a subdomain's south flag equals the north flag of the one below it, its east flag the west flag of the one to its right); 0 on faces at the grid's edge. `local_ops`: each subdomain's local dual operator is symmetric positive definite.
All inputs are finite; a program needn't handle non-finite values. No bound on the sum of `contact` on one device may be relied on, other than what follows from the above.
Results may differ from a plain program's by a relative error of at most 0.00099.
Values sent between devices are 32-bit elements; how exact they have to be, the bound alone decides.
A program may use at most 128 MiB of HBM per device.

v0:
```python
import functools

import jax
import jax.numpy as jnp
from jax import lax
from jax.sharding import Mesh
from jax.sharding import PartitionSpec as P

ITERS = 2
ROW = ("row_0", "row_1")
COL = ("col_0", "col_1", "col_2")
ROW_COL = ("row_0", "row_1", "col_0", "col_1", "col_2")


def extended(block, sides, width):
    for axis, dim in sides:
        count = lax.axis_size(axis)
        forward = [(i, i + 1) for i in range(count - 1)]
        backward = [(target, source) for source, target in forward]
        low = lax.ppermute(
            lax.slice_in_dim(block, block.shape[dim] - width, None, axis=dim), axis, forward
        )
        high = lax.ppermute(lax.slice_in_dim(block, 0, width, axis=dim), axis, backward)
        block = jnp.concatenate([low, block, high], axis=dim)
    return block


def in_blocks(value, dim, devices):
    shape = value.shape
    blocks = value.reshape(*shape[:dim], devices, shape[dim] // devices, *shape[dim + 1 :])
    return jnp.moveaxis(blocks, dim, 0)


def summed_on_arrival(value, axis, dim):
    blocks = in_blocks(value, dim, lax.axis_size(axis))
    arrived = lax.all_to_all(blocks, axis, split_axis=0, concat_axis=0, tiled=True)
    return arrived.sum(axis=0)


def by_axis(value, axes):
    return functools.reduce(lax.psum, axes, value)


def per_device(local_ops, loads, modes, coarse_inverse, face_rows, adjacency, contact):
    local_op = local_ops[0, 0]
    load_term = loads[0, 0]
    mode_rows = modes[0, 0]
    row_index = face_rows[0, 0]
    adj_flags = adjacency[0, 0].astype(jnp.float32)
    face_size = row_index.shape[1]
    order = load_term.shape[0]
    case_count = load_term.shape[1]
    flat_rows = row_index.reshape(-1)
    free_face = jnp.repeat(1.0 - adj_flags, face_size)
    row_free = jnp.zeros((order,), jnp.float32).at[flat_rows].set(free_face)
    weight = 0.5 + 0.5 * row_free
    clamp_rows = contact[0, 0].astype(jnp.float32) * row_free > 0.5

    def assemble(field_values):
        blocks = jnp.take(field_values, row_index, axis=0)
        vertical = extended(blocks[0:2], ((ROW, 0),), 1)
        lateral = extended(blocks[2:4], ((COL, 0),), 1)
        incoming = (
            jnp.stack([vertical[0], vertical[3], lateral[0], lateral[3]]) * adj_flags[:, None, None]
        )
        return field_values.at[flat_rows].add(incoming.reshape(-1, case_count))

    multipliers = jnp.zeros((order, case_count), jnp.float32)
    for iteration in range(ITERS):
        if iteration == 0:
            local_term = -load_term
        else:
            local_term = (
                jnp.dot(
                    local_op, multipliers.astype(jnp.bfloat16), preferred_element_type=jnp.float32
                )
                - load_term
            )
        gradient = assemble(local_term)
        coarse_coef = jnp.dot(
            mode_rows, gradient, precision=lax.Precision.HIGHEST, preferred_element_type=jnp.float32
        )
        tile_cols = coarse_inverse.shape[1]
        col_index = lax.axis_index(COL)
        gathered = lax.all_gather(coarse_coef, ROW_COL, axis=0, tiled=True)
        coarse_block = lax.dynamic_slice_in_dim(gathered, col_index * tile_cols, tile_cols, 0)
        coarse_amount = summed_on_arrival(
            jnp.dot(
                coarse_inverse,
                coarse_block,
                precision=lax.Precision.HIGHEST,
                preferred_element_type=jnp.float32,
            ),
            COL,
            0,
        )
        correction = lax.dot_general(
            mode_rows,
            coarse_amount,
            (((0,), (0,)), ((), ())),
            precision=lax.Precision.HIGHEST,
            preferred_element_type=jnp.float32,
        )
        direction = gradient - assemble(correction)
        direction_half = direction.astype(jnp.bfloat16)
        operated = jnp.dot(local_op, direction_half, preferred_element_type=jnp.float32)
        totals = (
            by_axis(jnp.sum(weight[:, None] * direction * direction, axis=0), ROW_COL),
            by_axis(jnp.sum(direction * operated, axis=0), ROW_COL),
        )
        step_length = totals[0] / totals[1]
        multipliers = multipliers - step_length[None, :] * direction
        multipliers = jnp.where(clamp_rows[:, None], jnp.maximum(multipliers, 0.0), multipliers)
    return multipliers[None, None]


def solution(mesh):
    torus = Mesh(mesh.devices.reshape(4, 2, 2, 4, 2), ("row_0", "row_1", "col_0", "col_1", "col_2"))
    return jax.shard_map(
        per_device,
        mesh=torus,
        in_specs=(
            P(ROW, COL, None, None),
            P(ROW, COL, None, None),
            P(ROW, COL, None, None),
            P(ROW, COL),
            P(ROW, COL, None, None),
            P(ROW, COL, None),
            P(ROW, COL, None),
        ),
        out_specs=P(ROW, COL, None, None),
        check_vma=False,
    )
```

profile of v0, /device:TPU:1, one launch (start us, length us, event | category | flops | bytes accessed | tf_op | source)
XLA Modules:
  0.0 553.5 jit_solution(13121661826302791065)
XLA Ops:
  14.7 8.6 %gather_fusion = f32[2048,256]{1,0:T(8,128)} fusion(f32[2048,256]{1,0:T(8,128)S(1)} %copy.45, s32[2048]{0:T(1024)S(1)} %broadcast_clamp_fusion), kind=kCustom, calls=%fused_computation.clone | custom fusion | bytes 4202496 | tf_op jit(solution)/shard_map/jit(_take)/gather | solution.py:60
  41.4 13.2 %collective-permute-done.1 = f32[1,512,256]{2,1,0:T(8,128)S(1)} collective-permute-done((f32[1,512,256]{2,1,0:T(8,128)S(1)}, f32[1,512,256]{2,1,0:T(8,128)S(1)}, u32[]{:S(2)}, u32[]{:S(2)}) %collective-permute-start.1) | collective-permute-done | bytes 524320 | tf_op jit(solution)/shard_map/ppermute | solution.py:23
  56.5 12.7 %scatter_fusion = f32[2048,256]{1,0:T(8,128)S(1)} fusion(f32[2048,256]{1,0:T(8,128)S(1)} %copy.45, s32[2048]{0:T(1024)S(1)} %bitcast.116, f32[2048,256]{1,0:T(8,128)} %bitcast_multiply_fusion.3), kind=kCustom, calls=%fused_computation.5 | custom fusion | flops 524288 | bytes 6299648 | tf_op jit(solution)/shard_map/scatter-add | solution.py:66
  71.1 73.4 %all-gather.3.cloned.1.call-done = f32[4096,256]{1,0:T(8,128)} async-done(((f32[32,256]{1,0:T(8,128)}), f32[4096,256]{1,0:T(8,128)}) %all-gather.3.cloned.1.call-update) | async-done | bytes 4194320 | tf_op jit(solution)/shard_map/all_gather | solution.py:85
  151.2 9.7 %all-to-all-done = f32[16,32,256]{2,1,0:T(8,128)S(1)} async-done(((f32[16,32,256]{2,1,0:T(8,128)}), f32[16,32,256]{2,1,0:T(8,128)S(1)}, u32[]{:S(2)}, u32[]{:S(2)}) %all-to-all-start) | async-done | bytes 524320 | tf_op jit(solution)/shard_map/all_to_all | solution.py:36
  167.0 10.1 %gather_fusion.1 = f32[2048,256]{1,0:T(8,128)} fusion(f32[2048,256]{1,0:T(8,128)} %copy.48, s32[2048]{0:T(1024)S(1)} %broadcast_clamp_fusion), kind=kCustom, calls=%fused_computation.1.clone | custom fusion | bytes 4202496 | tf_op jit(solution)/shard_map/jit(_take)/gather | solution.py:60
  191.7 8.5 %scatter_custom_fusion = f32[2048]{0:T(1024)S(1)} fusion(s32[2048]{0:T(1024)S(1)} %bitcast.117, f32[2048]{0:T(1024)S(1)} %bitcast.128, f32[]{:T(128)} %constant.19.clone.1), kind=kCustom, calls=%fused_computation.70 | custom fusion | bytes 8196 | tf_op jit(solution)/shard_map/scatter | solution.py:55
  211.1 12.7 %scatter_fusion.1 = f32[2048,256]{1,0:T(8,128)S(1)} fusion(f32[2048,256]{1,0:T(8,128)S(1)} %copy-done.1, s32[2048]{0:T(1024)S(1)} %bitcast.118, f32[2048,256]{1,0:T(8,128)} %bitcast_multiply_fusion.2), kind=kCustom, calls=%fused_computation.6 | custom fusion | flops 524288 | bytes 6299648 | tf_op jit(solution)/shard_map/scatter-add | solution.py:66
  228.3 6.7 %fusion.31 = f32[256]{0:T(256)S(1)} fusion(f32[2048,256]{0,1:T(8,128)S(1)} %get-tuple-element.29, bf16[1,1,2048,2048]{3,2,1,0:T(8,128)(2,1)} %param.9), kind=kOutput, calls=%fused_computation.41 | convolution fusion | flops 2149056256 | bytes 10486784 | tf_op jit(solution)/shard_map/dot_general | solution.py:106
  235.0 7.0 %all-reduce.3 = (f32[256]{0:T(256)S(1)}, f32[256]{0:T(256)S(1)}) all-reduce(f32[256]{0:T(256)S(1)} %get-tuple-element.28, f32[256]{0:T(256)S(1)} %fusion.31), channel_id=1, replica_groups=mesh['row_0'=4,'row_1'=2,'col_0'=2,'col_1'=4,'col_2'=2] {'row_0'}, use_global_device_ids=true, to_apply=%region_5.7 | all-reduce | flops 512 | bytes 4096 | tf_op jit(solution)/shard_map/psum | solution.py:41
  251.9 14.5 %all-reduce.1 = (f32[256]{0:T(256)S(1)}, f32[256]{0:T(256)S(1)}) all-reduce(f32[256]{0:T(256)S(1)} %get-tuple-element.20, f32[256]{0:T(256)S(1)} %get-tuple-element.21), channel_id=1, replica_groups=mesh['row_0'=4,'row_1'=2,'col_0'=2,'col_1'=4,'col_2'=2] {'col_1'}, use_global_device_ids=true, to_apply=%region_8.10 | all-reduce | flops 512 | bytes 4096 | tf_op jit(solution)/shard_map/psum | solution.py:41
  266.4 7.1 %all-reduce.5 = (f32[256]{0:T(256)S(1)}, f32[256]{0:T(256)S(1)}) all-reduce(f32[256]{0:T(256)S(1)} %get-tuple-element.8, f32[256]{0:T(256)S(1)} %get-tuple-element.9), channel_id=1, replica_groups=mesh['row_0'=4,'row_1'=2,'col_0'=2,'col_1'=4,'col_2'=2] {'col_2'}, use_global_device_ids=true, to_apply=%region_9.11 | all-reduce | flops 512 | bytes 4096 | tf_op jit(solution)/shard_map/psum | solution.py:41
  273.5 7.7 %fusion.21 = f32[2048,256]{0,1:T(8,128)} fusion(bf16[1,1,2048,2048]{3,2,1,0:T(8,128)(2,1)} %param.9, f32[1,1,2048,256]{2,3,1,0:T(8,128)S(1)} %copy-done.4, f32[2048,256]{0,1:T(8,128)} %copy-done.5, f32[256]{0:T(256)S(1)} %div.6, pred[2048]{0:T(1024)(128)(4,1)S(1)} %multiply_compare_fusion), kind=kOutput, calls=%fused_computation.26 | convolution fusion | flops 2150629376 | bytes 14683136 | tf_op jit(solution)/shard_map/dot_general | solution.py:74
  283.1 8.6 %gather_fusion.2 = f32[2048,256]{1,0:T(8,128)} fusion(f32[2048,256]{1,0:T(8,128)S(1)} %copy.52, s32[2048]{0:T(1024)S(1)} %broadcast_clamp_fusion), kind=kCustom, calls=%fused_computation.2.clone | custom fusion | bytes 4202496 | tf_op jit(solution)/shard_map/jit(_take)/gather | solution.py:60
  312.3 13.2 %collective-permute-done.9 = f32[1,512,256]{2,1,0:T(8,128)S(1)} collective-permute-done((f32[1,512,256]{2,1,0:T(8,128)S(1)}, f32[1,512,256]{2,1,0:T(8,128)S(1)}, u32[]{:S(2)}, u32[]{:S(2)}) %collective-permute-start.9) | collective-permute-done | bytes 524320 | tf_op jit(solution)/shard_map/ppermute | solution.py:23
  327.3 12.9 %scatter_fusion.2 = f32[2048,256]{1,0:T(8,128)S(1)} fusion(f32[2048,256]{1,0:T(8,128)S(1)} %copy.52, s32[2048]{0:T(1024)S(1)} %bitcast.119, f32[2048,256]{1,0:T(8,128)} %bitcast_multiply_fusion.1), kind=kCustom, calls=%fused_computation.7 | custom fusion | flops 524288 | bytes 6299648 | tf_op jit(solution)/shard_map/scatter-add | solution.py:66
  342.0 70.5 %all-gather.5.cloned.1.call-done = f32[4096,256]{1,0:T(8,128)} async-done(((f32[32,256]{1,0:T(8,128)}), f32[4096,256]{1,0:T(8,128)}) %all-gather.5.cloned.1.call-update) | async-done | bytes 4194320 | tf_op jit(solution)/shard_map/all_gather | solution.py:85
  415.5 13.4 %all_to_all.10 = f32[16,32,256]{2,1,0:T(8,128)S(1)} all-to-all(f32[16,32,256]{2,1,0:T(8,128)} %bitcast.115), channel_id=1, replica_groups=mesh['row_0'=4,'row_1'=2,'col_0'=2,'col_1'=4,'col_2'=2] {'col_0','col_1'..., dimensions={0} | all-to-all | bytes 1048576 | tf_op jit(solution)/shard_map/all_to_all | solution.py:36
  435.0 10.2 %gather_fusion.3 = f32[2048,256]{1,0:T(8,128)} fusion(f32[2048,256]{1,0:T(8,128)} %copy.55, s32[2048]{0:T(1024)S(1)} %broadcast_clamp_fusion), kind=kCustom, calls=%fused_computation.3.clone | custom fusion | bytes 4202496 | tf_op jit(solution)/shard_map/jit(_take)/gather | solution.py:60
  462.4 12.8 %collective-permute-done.13 = f32[1,512,256]{2,1,0:T(8,128)} collective-permute-done((f32[1,512,256]{2,1,0:T(8,128)}, f32[1,512,256]{2,1,0:T(8,128)}, u32[]{:S(2)}, u32[]{:S(2)}) %collective-permute-start.13) | collective-permute-done | bytes 524320 | tf_op jit(solution)/shard_map/ppermute | solution.py:23
  479.1 12.9 %scatter_fusion.3 = f32[2048,256]{1,0:T(8,128)S(1)} fusion(f32[2048,256]{1,0:T(8,128)S(1)} %copy-done.2, s32[2048]{0:T(1024)S(1)} %bitcast.120, f32[2048,256]{1,0:T(8,128)} %bitcast_multiply_fusion), kind=kCustom, calls=%fused_computation.8 | custom fusion | flops 524288 | bytes 6299648 | tf_op jit(solution)/shard_map/scatter-add | solution.py:66
  503.2 7.0 %all-reduce.2 = (f32[256]{0:T(256)S(1)}, f32[256]{0:T(256)S(1)}) all-reduce(f32[256]{0:T(256)S(1)} %get-tuple-element.26, f32[256]{0:T(256)S(1)} %fusion.28), channel_id=1, replica_groups=mesh['row_0'=4,'row_1'=2,'col_0'=2,'col_1'=4,'col_2'=2] {'row_0'}, use_global_device_ids=true, to_apply=%region_20.22 | all-reduce | flops 512 | bytes 4096 | tf_op jit(solution)/shard_map/psum | solution.py:41
  520.1 14.5 %all-reduce = (f32[256]{0:T(256)S(1)}, f32[256]{0:T(256)S(1)}) all-reduce(f32[256]{0:T(256)S(1)} %get-tuple-element.18, f32[256]{0:T(256)S(1)} %get-tuple-element.19), channel_id=1, replica_groups=mesh['row_0'=4,'row_1'=2,'col_0'=2,'col_1'=4,'col_2'=2] {'col_1'}, use_global_device_ids=true, to_apply=%region_23.25 | all-reduce | flops 512 | bytes 4096 | tf_op jit(solution)/shard_map/psum | solution.py:41
  534.5 7.1 %all-reduce.4 = (f32[256]{0:T(256)S(1)}, f32[256]{0:T(256)S(1)}) all-reduce(f32[256]{0:T(256)S(1)} %get-tuple-element.6, f32[256]{0:T(256)S(1)} %get-tuple-element.7), channel_id=1, replica_groups=mesh['row_0'=4,'row_1'=2,'col_0'=2,'col_1'=4,'col_2'=2] {'col_2'}, use_global_device_ids=true, to_apply=%region_24.26 | all-reduce | flops 512 | bytes 4096 | tf_op jit(solution)/shard_map/psum | solution.py:41
  (118 shorter events, 164.3 us)
Async XLA Ops:
  6.5 138.0 %copy-start = (f32[512,256]{1,0:T(8,128)S(1)}, f32[512,256]{1,0:T(8,128)}, u32[]{:S(2)}) copy-start(f32[512,256]{1,0:T(8,128)} %param.12) | copy-start | bytes 1572868
  6.5 138.0 %all-gather.3.cloned.1.call-start = ((), (), s32[]{:S(2)}) async-start(), calls=%async_computation.2 | async-start | bytes 4227072 | tf_op jit(solution)/shard_map/all_gather | solution.py:85
  25.2 13.3 %copy-start.10 = (s32[1,1,4]{2,1,0:T(1,128)S(1)}, s32[1,1,4]{2,1,0:T(1,128)}, u32[]{:S(2)}) copy-start(s32[1,1,4]{2,1,0:T(1,128)} %param.14) | copy-start | bytes 52
  25.2 13.4 %copy-start.8 = (s32[1,1,4,512]{3,2,1,0:T(4,128)S(1)}, s32[1,1,4,512]{3,2,1,0:T(4,128)}, u32[]{:S(2)}) copy-start(s32[1,1,4,512]{3,2,1,0:T(4,128)} %param.13) | copy-start | bytes 24580
  25.4 16.1 %collective-permute-start = (f32[1,512,256]{2,1,0:T(8,128)S(1)}, f32[1,512,256]{2,1,0:T(8,128)S(1)}, u32[]{:S(2)}, u32[]{:S(2)}) collective-permute-start(f32[1,512,256]{2,1,0:T(8,128)S(1)} %get-tuple-element.42), channel_id=1, source_target_pairs={{0,16},{16,32},{32,48},{48,64},{64,80},{80,96},{96,112},{1,17},{17... | collective-permute-start | bytes 1572872 | tf_op jit(solution)/shard_map/ppermute | solution.py:20
  30.9 23.8 %collective-permute-start.1 = (f32[1,512,256]{2,1,0:T(8,128)S(1)}, f32[1,512,256]{2,1,0:T(8,128)S(1)}, u32[]{:S(2)}, u32[]{:S(2)}) collective-permute-start(f32[1,512,256]{2,1,0:T(8,128)S(1)} %get-tuple-element.45), channel_id=1, source_target_pairs={{16,0},{32,16},{48,32},{64,48},{80,64},{96,80},{112,96},{17,1},{33... | collective-permute-start | bytes 1572872 | tf_op jit(solution)/shard_map/ppermute | solution.py:23
  32.2 22.5 %collective-permute-start.2 = (f32[1,512,256]{2,1,0:T(8,128)S(1)}, f32[1,512,256]{2,1,0:T(8,128)S(1)}, u32[]{:S(2)}, u32[]{:S(2)}) collective-permute-start(f32[1,512,256]{2,1,0:T(8,128)S(1)} %get-tuple-element.44), channel_id=1, source_target_pairs={{0,1},{1,2},{2,3},{3,4},{4,5},{5,6},{6,7},{7,8},{8,9},{9,10},{10,1... | collective-permute-start | bytes 1572872 | tf_op jit(solution)/shard_map/ppermute | solution.py:20
  36.6 18.1 %collective-permute-start.3 = (f32[1,512,256]{2,1,0:T(8,128)S(1)}, f32[1,512,256]{2,1,0:T(8,128)S(1)}, u32[]{:S(2)}, u32[]{:S(2)}) collective-permute-start(f32[1,512,256]{2,1,0:T(8,128)S(1)} %get-tuple-element.43), channel_id=1, source_target_pairs={{1,0},{2,1},{3,2},{4,3},{5,4},{6,5},{7,6},{8,7},{9,8},{10,9},{11,1... | collective-permute-start | bytes 1572872 | tf_op jit(solution)/shard_map/ppermute | solution.py:23
  147.5 13.4 %all-to-all-start = ((f32[16,32,256]{2,1,0:T(8,128)}), f32[16,32,256]{2,1,0:T(8,128)S(1)}, u32[]{:S(2)}, u32[]{:S(2)}) async-start(f32[16,32,256]{2,1,0:T(8,128)} %bitcast.114), calls=%async_computation | async-start | bytes 1048576 | tf_op jit(solution)/shard_map/all_to_all | solution.py:36
  151.2 261.3 %all-gather.5.cloned.1.call-start = ((), (), s32[]{:S(2)}) async-start(), calls=%async_computation.3 | async-start | bytes 4227072 | tf_op jit(solution)/shard_map/all_gather | solution.py:85
  179.1 21.2 %copy-start.9 = (s32[1,1,2048]{2,1,0:T(1,128)S(1)}, s32[1,1,2048]{2,1,0:T(1,128)}, u32[]{:S(2)}) copy-start(s32[1,1,2048]{2,1,0:T(1,128)} %param.15) | copy-start | bytes 24580
  180.3 21.8 %collective-permute-start.4 = (f32[1,512,256]{2,1,0:T(8,128)}, f32[1,512,256]{2,1,0:T(8,128)}, u32[]{:S(2)}, u32[]{:S(2)}) collective-permute-start(f32[1,512,256]{2,1,0:T(8,128)} %get-tuple-element.38), channel_id=1, source_target_pairs={{0,16},{16,32},{32,48},{48,64},{64,80},{80,96},{96,112},{1,17},{17... | collective-permute-start | bytes 1572872 | tf_op jit(solution)/shard_map/ppermute | solution.py:20
  184.8 22.3 %collective-permute-start.5 = (f32[1,512,256]{2,1,0:T(8,128)}, f32[1,512,256]{2,1,0:T(8,128)}, u32[]{:S(2)}, u32[]{:S(2)}) collective-permute-start(f32[1,512,256]{2,1,0:T(8,128)} %get-tuple-element.41), channel_id=1, source_target_pairs={{16,0},{32,16},{48,32},{64,48},{80,64},{96,80},{112,96},{17,1},{33... | collective-permute-start | bytes 1572872 | tf_op jit(solution)/shard_map/ppermute | solution.py:23
  186.1 21.0 %collective-permute-start.6 = (f32[1,512,256]{2,1,0:T(8,128)}, f32[1,512,256]{2,1,0:T(8,128)}, u32[]{:S(2)}, u32[]{:S(2)}) collective-permute-start(f32[1,512,256]{2,1,0:T(8,128)} %get-tuple-element.40), channel_id=1, source_target_pairs={{0,1},{1,2},{2,3},{3,4},{4,5},{5,6},{6,7},{7,8},{8,9},{9,10},{10,1... | collective-permute-start | bytes 1572872 | tf_op jit(solution)/shard_map/ppermute | solution.py:20
  188.0 19.1 %collective-permute-start.7 = (f32[1,512,256]{2,1,0:T(8,128)S(1)}, f32[1,512,256]{2,1,0:T(8,128)}, u32[]{:S(2)}, u32[]{:S(2)}) collective-permute-start(f32[1,512,256]{2,1,0:T(8,128)S(1)} %get-tuple-element.39), channel_id=1, source_target_pairs={{1,0},{2,1},{3,2},{4,3},{5,4},{6,5},{7,6},{8,7},{9,8},{10,9},{11,1... | collective-permute-start | bytes 1572872 | tf_op jit(solution)/shard_map/ppermute | solution.py:23
  228.3 45.2 %copy-start.4 = (f32[1,1,2048,256]{2,3,1,0:T(8,128)S(1)}, f32[1,1,2048,256]{2,3,1,0:T(8,128)}, u32[]{:S(2)}) copy-start(f32[1,1,2048,256]{2,3,1,0:T(8,128)} %copy-done.3) | copy-start | bytes 6291460
  293.8 10.0 %collective-permute-start.10 = (f32[1,512,256]{2,1,0:T(8,128)S(1)}, f32[1,512,256]{2,1,0:T(8,128)S(1)}, u32[]{:S(2)}, u32[]{:S(2)}) collective-permute-start(f32[1,512,256]{2,1,0:T(8,128)S(1)} %get-tuple-element.36), channel_id=1, source_target_pairs={{0,1},{1,2},{2,3},{3,4},{4,5},{5,6},{6,7},{7,8},{8,9},{9,10},{10,1... | collective-permute-start | bytes 1572872 | tf_op jit(solution)/shard_map/ppermute | solution.py:20
  297.7 10.5 %collective-permute-start.11 = (f32[1,512,256]{2,1,0:T(8,128)S(1)}, f32[1,512,256]{2,1,0:T(8,128)S(1)}, u32[]{:S(2)}, u32[]{:S(2)}) collective-permute-start(f32[1,512,256]{2,1,0:T(8,128)S(1)} %get-tuple-element.35), channel_id=1, source_target_pairs={{1,0},{2,1},{3,2},{4,3},{5,4},{6,5},{7,6},{8,7},{9,8},{10,9},{11,1... | collective-permute-start | bytes 1572872 | tf_op jit(solution)/shard_map/ppermute | solution.py:23
  299.6 12.7 %collective-permute-start.8 = (f32[1,512,256]{2,1,0:T(8,128)S(1)}, f32[1,512,256]{2,1,0:T(8,128)S(1)}, u32[]{:S(2)}, u32[]{:S(2)}) collective-permute-start(f32[1,512,256]{2,1,0:T(8,128)S(1)} %get-tuple-element.34), channel_id=1, source_target_pairs={{0,16},{16,32},{32,48},{48,64},{64,80},{80,96},{96,112},{1,17},{17... | collective-permute-start | bytes 1572872 | tf_op jit(solution)/shard_map/ppermute | solution.py:20
  302.2 23.3 %collective-permute-start.9 = (f32[1,512,256]{2,1,0:T(8,128)S(1)}, f32[1,512,256]{2,1,0:T(8,128)S(1)}, u32[]{:S(2)}, u32[]{:S(2)}) collective-permute-start(f32[1,512,256]{2,1,0:T(8,128)S(1)} %get-tuple-element.37), channel_id=1, source_target_pairs={{16,0},{32,16},{48,32},{64,48},{80,64},{96,80},{112,96},{17,1},{33... | collective-permute-start | bytes 1572872 | tf_op jit(solution)/shard_map/ppermute | solution.py:23
  448.3 14.1 %collective-permute-start.12 = (f32[1,512,256]{2,1,0:T(8,128)}, f32[1,512,256]{2,1,0:T(8,128)}, u32[]{:S(2)}, u32[]{:S(2)}) collective-permute-start(f32[1,512,256]{2,1,0:T(8,128)} %get-tuple-element.30), channel_id=1, source_target_pairs={{0,16},{16,32},{32,48},{48,64},{64,80},{80,96},{96,112},{1,17},{17... | collective-permute-start | bytes 1572872 | tf_op jit(solution)/shard_map/ppermute | solution.py:20
  452.8 22.3 %collective-permute-start.13 = (f32[1,512,256]{2,1,0:T(8,128)}, f32[1,512,256]{2,1,0:T(8,128)}, u32[]{:S(2)}, u32[]{:S(2)}) collective-permute-start(f32[1,512,256]{2,1,0:T(8,128)} %get-tuple-element.33), channel_id=1, source_target_pairs={{16,0},{32,16},{48,32},{64,48},{80,64},{96,80},{112,96},{17,1},{33... | collective-permute-start | bytes 1572872 | tf_op jit(solution)/shard_map/ppermute | solution.py:23
  454.1 21.0 %collective-permute-start.14 = (f32[1,512,256]{2,1,0:T(8,128)}, f32[1,512,256]{2,1,0:T(8,128)}, u32[]{:S(2)}, u32[]{:S(2)}) collective-permute-start(f32[1,512,256]{2,1,0:T(8,128)} %get-tuple-element.32), channel_id=1, source_target_pairs={{0,1},{1,2},{2,3},{3,4},{4,5},{5,6},{6,7},{7,8},{8,9},{9,10},{10,1... | collective-permute-start | bytes 1572872 | tf_op jit(solution)/shard_map/ppermute | solution.py:20
  456.1 19.1 %collective-permute-start.15 = (f32[1,512,256]{2,1,0:T(8,128)S(1)}, f32[1,512,256]{2,1,0:T(8,128)}, u32[]{:S(2)}, u32[]{:S(2)}) collective-permute-start(f32[1,512,256]{2,1,0:T(8,128)S(1)} %get-tuple-element.31), channel_id=1, source_target_pairs={{1,0},{2,1},{3,2},{4,3},{5,4},{6,5},{7,6},{8,7},{9,8},{10,9},{11,1... | collective-permute-start | bytes 1572872 | tf_op jit(solution)/shard_map/ppermute | solution.py:23
  (6 other events, 32.0 us)
Sparse Core Ops, SparseCore 0:
  71.2 73.2 all-gather.2
  342.1 70.3 all-gather.4
where the time goes:
time: 563 us; the launch traced here: 554 us
  waiting for transfers between devices  210 us (37%)
  blocking collectives  90.3 us (16%)
  other arithmetic  80.6 us (14%)
  local copies, waits for them, and re-layouts  74.2 us (13%)
  starting transfers between devices  49.1 us (9%)
  matrix products  35 us (6%)
  between operations  14.1 us (3%)
    all_gather x2, waiting for transfers between devices, per_device(): gathered = lax.all_gather(coarse_coef, ROW_COL, axis=0, tiled=True)  144 us
    psum x10, blocking collectives, by_axis(): return functools.reduce(lax.psum, axes, value)  76.9 us
    scatter-add x4, other arithmetic, assemble(): return field_values.at[flat_rows].add(incoming.reshape(-1, case_count))  51.3 us
    ppermute x8, waiting for transfers between devices, extended(): lax.ppermute(lax.slice_in_dim(block, 0, width, axis=dim), axis, backward)  48.5 us
    gather x4, local copies, waits for them, and re-layouts, assemble(): blocks = jnp.take(field_values, row_index, axis=0)  37.5 us
    ppermute x8, starting transfers between devices, extended(): lax.ppermute(lax.slice_in_dim(block, block.shape[dim] - width, None, axis...  29.2 us
    ppermute x8, starting transfers between devices, extended(): lax.ppermute(lax.slice_in_dim(block, 0, width, axis=dim), axis, backward)  16.2 us
    all_to_all x1, blocking collectives, summed_on_arrival(): lax.all_to_all(blocks, axis, split_axis=0, concat_axis=0, tiled=True)  13.4 us
  transfers between devices with their start and end apart: 19, of which 12 were waited for; matrix products, arithmetic and copies ran while one was open for 2% of the time, Pallas kernels for 0%

commit v1 on v0

v1 whole, which is shorter than its diff:
```python
import functools

import jax
import jax.numpy as jnp
from jax import lax
from jax.experimental import pallas as pl
from jax.experimental.pallas import tpu as pltpu
from jax.sharding import PartitionSpec as P

ITERS = 2
F32 = jnp.float32
BF16 = jnp.bfloat16
MESH = pl.DeviceIdType.MESH
LANES = 128
VMEM_BYTES = 63_000_000


def halves(value):
    high = value.astype(BF16)
    low = (value - high.astype(F32)).astype(BF16)
    return high, low


def mul(a, b):
    return jnp.dot(a, b, preferred_element_type=F32)


def mul_split(a, b):
    a_high, a_low = a
    b_high, b_low = b
    return mul(a_high, b_high) + (mul(a_high, b_low) + mul(a_low, b_high))


def wide(value):
    return jnp.concatenate([value, value], axis=1)


def by_eight(value):
    return value.reshape(value.shape[0] // 8, 8, value.shape[1]).sum(axis=0)


def kernel(
    rows,
    cols,
    adj_ref,
    modes_ref,
    loads_ref,
    tile_ref,
    index_ref,
    contact_ref,
    op_hbm,
    out_ref,
    op_ref,
    pick,
    place,
    pieces,
    modes_high,
    modes_low,
    modes_high_t,
    modes_low_t,
    row_weight,
    row_clamp,
    field,
    direction,
    direction_half,
    mode_send,
    mode_recv,
    face_send,
    face_recv,
    product_send,
    product_recv,
    coef_send,
    coef_recv,
    part_send,
    part_recv,
    amount_send,
    amount_recv,
    first_send,
    first_recv,
    second_send,
    second_recv,
    op_sem,
    mode_sems,
    face_sems,
    product_sems,
    coef_sems,
    part_sems,
    amount_sems,
    first_sems,
    second_sems,
):
    row = lax.axis_index("row")
    col = lax.axis_index("col")
    order, cases = loads_ref.shape
    mode_count = modes_ref.shape[0]
    face = index_ref.shape[1]
    group = coef_recv.shape[1]
    step = 512
    blocks = order // step

    op_copy = pltpu.make_async_copy(op_hbm, op_ref, op_sem)
    op_copy.start()

    sides = (
        (row > 0, (row - 1, col)),
        (row < rows - 1, (row + 1, col)),
        (col > 0, (row, col - 1)),
        (col < cols - 1, (row, col + 1)),
    )
    coef_col = (row * cols + col) // group
    coef_slot = lax.rem(col, group)
    source_row = (col * group) // cols
    source_col = lax.rem(col * group, cols)
    at_home = coef_col == col

    barrier = pltpu.get_barrier_semaphore()
    for k in range(1, cols):
        pl.semaphore_signal(
            barrier, inc=1, device_id=(row, lax.rem(col + k, cols)), device_id_type=MESH
        )
    for k in range(1, rows):
        pl.semaphore_signal(
            barrier, inc=1, device_id=(lax.rem(row + k, rows), col), device_id_type=MESH
        )
    for k in range(group):
        is_me = (source_row == row) & (source_col + k == col)

        @pl.when(jnp.logical_not(is_me))
        def _():
            pl.semaphore_signal(
                barrier, inc=1, device_id=(source_row, source_col + k), device_id_type=MESH
            )

    for f in range(4):

        @pl.when(jnp.logical_not(sides[f][0]))
        def _():
            mode_recv[f] = jnp.zeros(mode_recv.shape[1:], F32)
            for it in range(ITERS):
                face_recv[it, f] = jnp.zeros(face_recv.shape[2:], F32)
                product_recv[it, f] = jnp.zeros(product_recv.shape[2:], F32)
                amount_recv[it, f] = jnp.zeros(amount_recv.shape[2:], F32)

    def side_copy(f, source, target, sems):
        return pltpu.make_async_remote_copy(
            src_ref=source,
            dst_ref=target.at[f ^ 1],
            send_sem=sems.at[0, f],
            recv_sem=sems.at[1, f ^ 1],
            device_id=sides[f][1],
            device_id_type=MESH,
        )

    def start_side(f, source, target, sems):
        @pl.when(sides[f][0])
        def _():
            side_copy(f, source, target, sems).start()

    def wait_side(f, target, sems):
        @pl.when(sides[f][0])
        def _():
            pltpu.make_async_remote_copy(
                src_ref=target.at[f],
                dst_ref=target.at[f],
                send_sem=sems.at[0, f],
                recv_sem=sems.at[1, f],
                device_id=sides[f][1],
                device_id_type=MESH,
            ).wait_recv()

    def sent_side(f, source, target, sems):
        @pl.when(sides[f][0])
        def _():
            side_copy(f, source, target, sems).wait_send()

    @pl.loop(0, order // 256)
    def _(i):
        at = pl.ds(pl.multiple_of(i * 256, 256), 256)
        for f in range(4):
            here = lax.broadcasted_iota(jnp.int32, (256, face), 0) + i * 256
            hit = here == index_ref[f : f + 1, :]
            place[at, f * face : (f + 1) * face] = jnp.where(hit, 1.0, 0.0).astype(BF16)

    high, low = halves(modes_ref[...])
    modes_high[0:mode_count] = high
    modes_low[0:mode_count] = low
    both = jnp.concatenate([high, low], axis=0)
    for f in range(4):
        moved = mul(both, place[:, f * face : (f + 1) * face])
        mode_send[f] = moved[0:mode_count] + moved[mode_count:]

    here = (source_row == row) & (source_col <= col) & (col < source_col + group)
    pl.semaphore_wait(barrier, cols - 1 + rows - 1 + group - here.astype(jnp.int32))
    for f in range(4):
        start_side(f, mode_send.at[f], mode_recv, mode_sems)

    for f in range(4):
        down = jnp.broadcast_to(index_ref[f : f + 1, :], (LANES, face)).T

        @pl.loop(0, order // LANES)
        def _(i):
            there = lax.broadcasted_iota(jnp.int32, (face, LANES), 1) + i * LANES
            at = pl.ds(pl.multiple_of(i * LANES, LANES), LANES)
            pick[f * face : (f + 1) * face, at] = jnp.where(down == there, 1.0, 0.0).astype(BF16)

    def each_block(body):
        @pl.loop(0, blocks)
        def _(i):
            body(pl.ds(pl.multiple_of(i * step, step), step))

    def negate(at):
        value = -loads_ref[at, :]
        field[at, :] = value
        high, low = halves(value)
        pieces[at, 0:cases] = high
        pieces[at, cases:] = low

    def faces_of_field(it):
        for f in range(4):
            moved = mul(pick[f * face : (f + 1) * face, :], pieces[...])
            face_send[it, f] = moved[:, 0:cases] + moved[:, cases:]

    def flag(f):
        return adj_ref[0, f].astype(F32)

    def fill_modes():
        for f in range(4):
            high, low = halves(mode_recv[f])
            moved = mul(
                jnp.concatenate([high, low], axis=0), pick[f * face : (f + 1) * face, :]
            )
            high, low = halves(moved[0:mode_count] + moved[mode_count:])
            at = slice((f + 1) * mode_count, (f + 2) * mode_count)
            modes_high[at] = high
            modes_low[at] = low
        modes_high_t[...] = modes_high[...].astype(F32).T.astype(BF16)
        modes_low_t[...] = modes_low[...].astype(F32).T.astype(BF16)

    def fill_rows():
        flags = jnp.concatenate(
            [jnp.full((face, LANES), flag(f), F32) for f in range(4)], axis=0
        ).astype(BF16)
        for i in range(blocks):
            glued = mul(place[i * step : (i + 1) * step, :], flags)
            touching = (
                jnp.broadcast_to(contact_ref[:, i * step : (i + 1) * step], (LANES, step))
                .astype(F32)
                .T
            )
            free = 1.0 - glued
            row_weight[i * step : (i + 1) * step, :] = 0.5 + 0.5 * free
            row_clamp[i * step : (i + 1) * step, :] = touching * free

    def clamped(at, value):
        return jnp.where(wide(row_clamp[at, :]) > 0.5, jnp.maximum(value, 0.0), value)

    def all_sum(it, totals):
        parts = cases // LANES
        tile = jnp.concatenate(
            [totals[t : t + 1, p * LANES : (p + 1) * LANES] for t in range(2) for p in range(parts)]
            + [jnp.zeros((8 - 2 * parts, LANES), F32)],
            axis=0,
        )
        first_send[it] = tile

        def first(k):
            return pltpu.make_async_remote_copy(
                src_ref=first_send.at[it],
                dst_ref=first_recv.at[it, k],
                send_sem=first_sems.at[it, 0, k],
                recv_sem=first_sems.at[it, 1, k],
                device_id=(row, lax.rem(col + k, cols)),
                device_id_type=MESH,
            )

        for k in range(1, cols):
            first(k).start()
        for k in range(1, cols):
            first(k).wait_recv()
        tile = tile + first_recv[it, 1:cols].sum(axis=0)
        second_send[it] = tile

        def second(k):
            return pltpu.make_async_remote_copy(
                src_ref=second_send.at[it],
                dst_ref=second_recv.at[it, k],
                send_sem=second_sems.at[it, 0, k],
                recv_sem=second_sems.at[it, 1, k],
                device_id=(lax.rem(row + k, rows), col),
                device_id_type=MESH,
            )

        for k in range(1, rows):
            second(k).start()
        for k in range(1, rows):
            second(k).wait_recv()
        tile = tile + second_recv[it, 1:rows].sum(axis=0)
        for k in range(1, cols):
            first(k).wait_send()
        for k in range(1, rows):
            second(k).wait_send()
        top = jnp.concatenate([tile[p : p + 1] for p in range(parts)], axis=1)
        low = jnp.concatenate([tile[parts + p : parts + p + 1] for p in range(parts)], axis=1)
        return top / low

    for it in range(ITERS):
        if it == 0:
            each_block(negate)
            faces_of_field(it)
            for f in range(4):
                wait_side(f, mode_recv, mode_sems)
            for f in range(4):
                mode_recv[f] = mode_recv[f] * flag(f)
            for f in range(4):
                product_send[it, f] = mul_split(halves(mode_recv[f]), halves(face_send[it, f]))
            for f in range(4):
                start_side(f, product_send.at[it, f], product_recv.at[it], product_sems.at[it])
            own = mul_split(
                (modes_high[0:mode_count], modes_low[0:mode_count]),
                (pieces[:, 0:cases], pieces[:, cases:]),
            )
        else:
            products = mul_split(
                (modes_high[...], modes_low[...]), (pieces[:, 0:cases], pieces[:, cases:])
            )
            own = products[0:mode_count]
            for f in range(4):
                product_send[it, f] = products[(f + 1) * mode_count : (f + 2) * mode_count]
            for f in range(4):
                start_side(f, product_send.at[it, f], product_recv.at[it], product_sems.at[it])
            faces_of_field(it)
        for f in range(4):
            wait_side(f, product_recv.at[it], product_sems.at[it])
            own = own + product_recv[it, f]
        coef_send[it] = own

        def coef(k):
            return pltpu.make_async_remote_copy(
                src_ref=coef_send.at[it],
                dst_ref=coef_recv.at[it, coef_slot],
                send_sem=coef_sems.at[it, 0, k],
                recv_sem=coef_sems.at[it, 1, coef_slot],
                device_id=(lax.rem(row + k, rows), coef_col),
                device_id_type=MESH,
            )

        for k in range(rows):
            if k == 0:

                @pl.when(at_home)
                def _():
                    coef_recv[it, coef_slot] = own

                @pl.when(jnp.logical_not(at_home))
                def _():
                    coef(0).start()

            else:
                coef(k).start()
        for f in range(4):
            start_side(f, face_send.at[it, f], face_recv.at[it], face_sems.at[it])
        if it == 0:
            fill_modes()
            fill_rows()
        for k in range(group):
            is_me = (source_row == row) & (source_col + k == col)

            @pl.when(jnp.logical_not(is_me))
            def _():
                pltpu.make_async_remote_copy(
                    src_ref=coef_send.at[it],
                    dst_ref=coef_recv.at[it, k],
                    send_sem=coef_sems.at[it, 0, 0],
                    recv_sem=coef_sems.at[it, 1, k],
                    device_id=(source_row, source_col + k),
                    device_id_type=MESH,
                ).wait_recv()

        block = coef_recv[it].reshape(group * mode_count, cases)
        part_send[it] = mul_split(halves(tile_ref[...]), halves(block)).reshape(
            cols, mode_count, cases
        )

        def part(k):
            target = lax.rem(col + k, cols)
            return pltpu.make_async_remote_copy(
                src_ref=part_send.at[it, target],
                dst_ref=part_recv.at[it, k],
                send_sem=part_sems.at[it, 0, k],
                recv_sem=part_sems.at[it, 1, k],
                device_id=(row, target),
                device_id_type=MESH,
            )

        for k in range(1, cols):
            part(k).start()
        for k in range(1, cols):
            part(k).wait_recv()
        amount = part_send[it, col] + part_recv[it, 1:cols].sum(axis=0)
        amount_send[it] = amount
        for f in range(4):
            start_side(f, amount_send.at[it], amount_recv.at[it], amount_sems.at[it])

        for f in range(4):
            wait_side(f, face_recv.at[it], face_sems.at[it])
            high, low = halves(face_recv[it, f] * flag(f))
            pieces[f * face : (f + 1) * face, 0:cases] = high
            pieces[f * face : (f + 1) * face, cases:] = low

        def add_faces(at):
            moved = mul(place[at, :], pieces[...])
            field[at, :] = field[at, :] + (moved[:, 0:cases] + moved[:, cases:])

        each_block(add_faces)
        for f in range(4):
            wait_side(f, amount_recv.at[it], amount_sems.at[it])
        amounts = halves(
            jnp.concatenate([amount] + [amount_recv[it, f] for f in range(4)], axis=0)
        )

        def turn(i, total):
            at = pl.ds(pl.multiple_of(i * step, step), step)
            value = field[at, :] - mul_split((modes_high_t[at, :], modes_low_t[at, :]), amounts)
            direction[at, :] = value
            direction_half[at, :] = value.astype(BF16)
            return total + by_eight(wide(row_weight[at, :]) * value * value)

        top = lax.fori_loop(0, blocks, turn, jnp.zeros((8, cases), F32))
        if it == 0:
            op_copy.wait()

        def operate(i, total):
            at = pl.ds(pl.multiple_of(i * step, step), step)
            return total + by_eight(direction[at, :] * mul(op_ref[at, :], direction_half[...]))

        low = lax.fori_loop(0, blocks, operate, jnp.zeros((8, cases), F32))
        totals = jnp.concatenate(
            [top.sum(axis=0, keepdims=True), low.sum(axis=0, keepdims=True)], axis=0
        )
        length = all_sum(it, totals)

        if it == 0:

            def first_update(at):
                value = clamped(at, 0.0 - length * direction[at, :])
                out_ref[at, :] = value
                direction_half[at, :] = value.astype(BF16)

            each_block(first_update)

            def local_term(at):
                value = mul(op_ref[at, :], direction_half[...]) - loads_ref[at, :]
                field[at, :] = value
                high, low = halves(value)
                pieces[at, 0:cases] = high
                pieces[at, cases:] = low

            each_block(local_term)
        else:

            def last_update(at):
                out_ref[at, :] = clamped(at, out_ref[at, :] - length * direction[at, :])

            each_block(last_update)

        for f in range(4):
            if it == 0:
                sent_side(f, mode_send.at[f], mode_recv, mode_sems)
            sent_side(f, product_send.at[it, f], product_recv.at[it], product_sems.at[it])
            sent_side(f, face_send.at[it, f], face_recv.at[it], face_sems.at[it])
            sent_side(f, amount_send.at[it], amount_recv.at[it], amount_sems.at[it])
        for k in range(rows):
            if k == 0:

                @pl.when(jnp.logical_not(at_home))
                def _():
                    coef(0).wait_send()

            else:
                coef(k).wait_send()
        for k in range(1, cols):
            part(k).wait_send()


def per_device(rows, cols, local_ops, loads, modes, coarse_inverse, face_rows, adjacency, contact):
    order, cases = loads.shape[2:]
    mode_count = modes.shape[2]
    face = face_rows.shape[3]
    group = coarse_inverse.shape[1] // mode_count
    stack = 5 * mode_count
    vmem = pl.BlockSpec(memory_space=pltpu.VMEM)
    dma = pltpu.SemaphoreType.DMA
    scratch = [
        pltpu.VMEM((order, order), BF16),
        pltpu.VMEM((order, order), BF16),
        pltpu.VMEM((order, order), BF16),
        pltpu.VMEM((order, 2 * cases), BF16),
        pltpu.VMEM((stack, order), BF16),
        pltpu.VMEM((stack, order), BF16),
        pltpu.VMEM((order, stack), BF16),
        pltpu.VMEM((order, stack), BF16),
        pltpu.VMEM((order, LANES), F32),
        pltpu.VMEM((order, LANES), F32),
        pltpu.VMEM((order, cases), F32),
        pltpu.VMEM((order, cases), F32),
        pltpu.VMEM((order, cases), BF16),
        pltpu.VMEM((4, mode_count, face), F32),
        pltpu.VMEM((4, mode_count, face), F32),
        pltpu.VMEM((ITERS, 4, face, cases), F32),
        pltpu.VMEM((ITERS, 4, face, cases), F32),
        pltpu.VMEM((ITERS, 4, mode_count, cases), F32),
        pltpu.VMEM((ITERS, 4, mode_count, cases), F32),
        pltpu.VMEM((ITERS, mode_count, cases), F32),
        pltpu.VMEM((ITERS, group, mode_count, cases), F32),
        pltpu.VMEM((ITERS, cols, mode_count, cases), F32),
        pltpu.VMEM((ITERS, cols, mode_count, cases), F32),
        pltpu.VMEM((ITERS, mode_count, cases), F32),
        pltpu.VMEM((ITERS, 4, mode_count, cases), F32),
        pltpu.VMEM((ITERS, 8, LANES), F32),
        pltpu.VMEM((ITERS, cols, 8, LANES), F32),
        pltpu.VMEM((ITERS, 8, LANES), F32),
        pltpu.VMEM((ITERS, rows, 8, LANES), F32),
        dma,
        dma((2, 4)),
        dma((ITERS, 2, 4)),
        dma((ITERS, 2, 4)),
        dma((ITERS, 2, max(rows, group))),
        dma((ITERS, 2, cols)),
        dma((ITERS, 2, 4)),
        dma((ITERS, 2, cols)),
        dma((ITERS, 2, rows)),
    ]
    result = pl.pallas_call(
        functools.partial(kernel, rows, cols),
        out_shape=jax.ShapeDtypeStruct((order, cases), F32),
        in_specs=[pl.BlockSpec(memory_space=pltpu.SMEM)]
        + [vmem] * 5
        + [pl.BlockSpec(memory_space=pl.ANY)],
        out_specs=vmem,
        scratch_shapes=scratch,
        compiler_params=pltpu.CompilerParams(
            collective_id=0, has_side_effects=True, vmem_limit_bytes=VMEM_BYTES
        ),
        name="dual_steps",
    )(
        adjacency[0],
        modes[0, 0],
        loads[0, 0],
        coarse_inverse,
        face_rows[0, 0],
        contact[0],
        local_ops[0, 0],
    )
    return result[None, None]


def solution(mesh):
    rows, cols = mesh.shape["row"], mesh.shape["col"]
    return jax.shard_map(
        functools.partial(per_device, rows, cols),
        mesh=mesh,
        in_specs=(
            P("row", "col", None, None),
            P("row", "col", None, None),
            P("row", "col", None, None),
            P("row", "col"),
            P("row", "col", None, None),
            P("row", "col", None),
            P("row", "col", None),
        ),
        out_specs=P("row", "col", None, None),
        check_vma=False,
    )
```

time: 563 us -> 157 us (0.28); the launches traced: 554 us -> 157 us
  waiting for transfers between devices: 210 us -> 0 us
  Pallas kernels: 0 us -> 154 us
  blocking collectives: 90.3 us -> 0 us
  other arithmetic: 80.6 us -> 0 us
  local copies, waits for them, and re-layouts: 74.2 us -> 3.05 us
  starting transfers between devices: 49.1 us -> 0 us
  matrix products: 35 us -> 0 us
  between operations: 14.1 us -> 0.01 us
    pallas_call x0 -> x1, Pallas kernels: none -> 154 us  [per_device(): pl.pallas_call(functools.partial(kernel, rows, cols), out_shape=jax.Shape...]
    all_gather x2 -> x0, waiting for transfers between devices: 144 us -> none  [per_device(): gathered = lax.all_gather(coarse_coef, ROW_COL, axis=0, tiled=True)]
    psum x10 -> x0, blocking collectives: 76.9 us -> none  [by_axis(): return functools.reduce(lax.psum, axes, value)]
    ppermute x16 -> x0, waiting for transfers between devices: 56.6 us -> none  [the longest x8 48.5 us: extended(): lax.ppermute(lax.slice_in_dim(block, 0, width, axis=dim), axis, backward)]
    scatter-add x4 -> x0, other arithmetic: 51.3 us -> none  [assemble(): return field_values.at[flat_rows].add(incoming.reshape(-1, case_count))]
    ppermute x16 -> x0, starting transfers between devices: 45.4 us -> none  [the longest x8 29.2 us: extended(): lax.ppermute(lax.slice_in_dim(block, block.shape[dim] - width, None, axis...]
    gather x4 -> x0, local copies, waits for them, and re-layouts: 37.5 us -> none  [assemble(): blocks = jnp.take(field_values, row_index, axis=0)]
    dot_general x9 -> x0, matrix products: 35 us -> none  [the longest x2 13.4 us: per_device(): jnp.dot(local_op, direction_half, preferred_element_type=jnp.float32)]
  transfers between devices with their start and end apart: 19 -> 0, of which waited for: 12 -> 0; matrix products, arithmetic and copies ran while one was open for 2% -> 0% of each run, Pallas kernels for 0% -> 0%
where the time goes in v1:
time: 157 us
  Pallas kernels  154 us (98%)
  local copies, waits for them, and re-layouts  3.05 us (2%)
    pallas_call x1, Pallas kernels, per_device(): pl.pallas_call(functools.partial(kernel, rows, cols), out_shape=jax.Shape...  154 us

profile of v1, /device:TPU:1, one launch (start us, length us, event | category | flops | bytes accessed | tf_op | source)
XLA Modules:
  0.0 156.8 jit_solution(7941558850043267070)
XLA Ops:
  0.0 153.8 %dual_steps.1 = f32[2048,256]{1,0:T(8,128)} custom-call(s32[1,4]{1,0:T(1,128)} %bitcast.13, f32[32,2048]{1,0:T(8,128)} %bitcast.10, f32[2048,256]{1,0:T(8,128)} %bitcast.9, f32[512,256]{1,0:T(8,128)} %tile_ref.1, s32[4,512]{1,0:T(4,128)} %bitcast.11, s32[1,2048]{1,0:T(1,128)} %bitcast.12, bf16[2048,2048]{1,0:T(8,128)(2,1)} %bitcast.7), custom_call_target="tpu_custom_call" | custom-call | tf_op jit(solution)/shard_map/dual_steps/pallas_call | solution.py:533
  153.8 3.0 %copy.9 = f32[1,1,2048,256]{3,2,1,0:T(8,128)} copy(f32[1,1,2048,256]{3,2,1,0:T(8,128)} %bitcast.8) | data formatting | bytes 4194304

commit v2 on v1

--- a/solution.py
+++ b/solution.py
@@ -13,6 +13,12 @@
 MESH = pl.DeviceIdType.MESH
 LANES = 128
 VMEM_BYTES = 63_000_000
+TICKS = 8
+SCHEDULE = (
+    {"faces": (0, 1), "sides": (2,), "products": (3,), "coefs": (4, 5), "parts": (6, 7)},
+    {"faces": (0, 1), "coefs": (2, 3), "parts": (4, 5, 6, 7)},
+)
+LOWEST = float(jnp.finfo(jnp.float32).min)
 
 
 def halves(value):
@@ -44,22 +50,26 @@
     cols,
     adj_ref,
     modes_ref,
+    index_ref,
+    contact_ref,
+    loads_hbm,
+    tile_hbm,
+    op_hbm,
+    out_hbm,
     loads_ref,
     tile_ref,
-    index_ref,
-    contact_ref,
-    op_hbm,
-    out_ref,
     op_ref,
     pick,
     place,
+    face_op,
     pieces,
     modes_high,
     modes_low,
     modes_high_t,
     modes_low_t,
     row_weight,
-    row_clamp,
+    row_floor,
+    first_value,
     field,
     direction,
     direction_half,
@@ -72,6 +82,8 @@
     coef_send,
     coef_recv,
     part_send,
+    pair_recv,
+    pair_send,
     part_recv,
     amount_send,
     amount_recv,
@@ -79,11 +91,13 @@
     first_recv,
     second_send,
     second_recv,
-    op_sem,
+    local_sems,
     mode_sems,
     face_sems,
+    strip_sems,
     product_sems,
     coef_sems,
+    pair_sems,
     part_sems,
     amount_sems,
     first_sems,
@@ -98,7 +112,11 @@
     step = 512
     blocks = order // step
 
-    op_copy = pltpu.make_async_copy(op_hbm, op_ref, op_sem)
+    loads_copy = pltpu.make_async_copy(loads_hbm, loads_ref, local_sems.at[0])
+    tile_copy = pltpu.make_async_copy(tile_hbm, tile_ref, local_sems.at[1])
+    op_copy = pltpu.make_async_copy(op_hbm, op_ref, local_sems.at[2])
+    loads_copy.start()
+    tile_copy.start()
     op_copy.start()
 
     sides = (
@@ -136,8 +154,8 @@
         @pl.when(jnp.logical_not(sides[f][0]))
         def _():
             mode_recv[f] = jnp.zeros(mode_recv.shape[1:], F32)
+            face_recv[f] = jnp.zeros(face_recv.shape[1:], F32)
             for it in range(ITERS):
-                face_recv[it, f] = jnp.zeros(face_recv.shape[2:], F32)
                 product_recv[it, f] = jnp.zeros(product_recv.shape[2:], F32)
                 amount_recv[it, f] = jnp.zeros(amount_recv.shape[2:], F32)
 
@@ -173,35 +191,99 @@
         def _():
             side_copy(f, source, target, sems).wait_send()
 
-    @pl.loop(0, order // 256)
-    def _(i):
-        at = pl.ds(pl.multiple_of(i * 256, 256), 256)
+    def fill_pick(faces):
+        for f in faces:
+            down = jnp.broadcast_to(index_ref[f : f + 1, :], (LANES, face)).T
+
+            @pl.loop(0, order // LANES)
+            def _(i):
+                there = lax.broadcasted_iota(jnp.int32, (face, LANES), 1) + i * LANES
+                at = pl.ds(pl.multiple_of(i * LANES, LANES), LANES)
+                pick[f * face : (f + 1) * face, at] = jnp.where(down == there, 1.0, 0.0).astype(
+                    BF16
+                )
+
+    def send_modes():
+        high, low = halves(modes_ref[...])
+        modes_high[0:mode_count] = high
+        modes_low[0:mode_count] = low
+        both = jnp.concatenate([high, low], axis=0)
         for f in range(4):
-            here = lax.broadcasted_iota(jnp.int32, (256, face), 0) + i * 256
-            hit = here == index_ref[f : f + 1, :]
-            place[at, f * face : (f + 1) * face] = jnp.where(hit, 1.0, 0.0).astype(BF16)
-
-    high, low = halves(modes_ref[...])
-    modes_high[0:mode_count] = high
-    modes_low[0:mode_count] = low
-    both = jnp.concatenate([high, low], axis=0)
-    for f in range(4):
-        moved = mul(both, place[:, f * face : (f + 1) * face])
-        mode_send[f] = moved[0:mode_count] + moved[mode_count:]
-
-    here = (source_row == row) & (source_col <= col) & (col < source_col + group)
-    pl.semaphore_wait(barrier, cols - 1 + rows - 1 + group - here.astype(jnp.int32))
-    for f in range(4):
-        start_side(f, mode_send.at[f], mode_recv, mode_sems)
-
-    for f in range(4):
-        down = jnp.broadcast_to(index_ref[f : f + 1, :], (LANES, face)).T
-
-        @pl.loop(0, order // LANES)
+            moved = lax.dot_general(
+                both,
+                pick[f * face : (f + 1) * face, :],
+                (((1,), (1,)), ((), ())),
+                preferred_element_type=F32,
+            )
+            mode_send[f] = moved[0:mode_count] + moved[mode_count:]
+        for f in range(4):
+            start_side(f, mode_send.at[f], mode_recv, mode_sems)
+
+    def greet():
+        here = (source_row == row) & (source_col <= col) & (col < source_col + group)
+        greeted = cols - 1 + rows - 1 + group - here.astype(jnp.int32)
+        pl.semaphore_wait(barrier, greeted)
+
+    def pick_op(f):
+        @pl.loop(0, order // step)
         def _(i):
-            there = lax.broadcasted_iota(jnp.int32, (face, LANES), 1) + i * LANES
-            at = pl.ds(pl.multiple_of(i * LANES, LANES), LANES)
-            pick[f * face : (f + 1) * face, at] = jnp.where(down == there, 1.0, 0.0).astype(BF16)
+            at = pl.ds(pl.multiple_of(i * step, step), step)
+            face_op[f * face : (f + 1) * face, at] = mul(
+                pick[f * face : (f + 1) * face, :], op_ref[:, at]
+            ).astype(BF16)
+
+    def fill_place():
+        @pl.loop(0, order // 256)
+        def _(i):
+            at = pl.ds(pl.multiple_of(i * 256, 256), 256)
+            for f in range(4):
+                here = lax.broadcasted_iota(jnp.int32, (256, face), 0) + i * 256
+                hit = here == index_ref[f : f + 1, :]
+                place[at, f * face : (f + 1) * face] = jnp.where(hit, 1.0, 0.0).astype(BF16)
+
+    def strip(it, f, j, incoming):
+        tall = face // TICKS
+        at = pl.ds(j * tall, tall)
+        if incoming:
+            source = face_recv.at[f, at]
+            target = source
+            arrived = f
+        else:
+            source = face_send.at[f, at]
+            target = face_recv.at[f ^ 1, at]
+            arrived = f ^ 1
+        return pltpu.make_async_remote_copy(
+            src_ref=source,
+            dst_ref=target,
+            send_sem=strip_sems.at[0, f, j],
+            recv_sem=strip_sems.at[1, arrived, j],
+            device_id=sides[f][1],
+            device_id_type=MESH,
+        )
+
+    def tick(it, point):
+        for j in SCHEDULE[it].get(point, ()):
+            for f in range(2):
+
+                @pl.when(sides[f][0])
+                def _():
+                    strip(it, f, j, False).start()
+
+    def wait_strips(it, *ticks):
+        for j in ticks:
+            for f in range(2):
+
+                @pl.when(sides[f][0])
+                def _():
+                    strip(it, f, j, True).wait_recv()
+
+    def sent_strips(it):
+        for j in range(TICKS):
+            for f in range(2):
+
+                @pl.when(sides[f][0])
+                def _():
+                    strip(it, f, j, False).wait_send()
 
     def each_block(body):
         @pl.loop(0, blocks)
@@ -215,10 +297,10 @@
         pieces[at, 0:cases] = high
         pieces[at, cases:] = low
 
-    def faces_of_field(it):
-        for f in range(4):
+    def faces_of_field(it, faces):
+        for f in faces:
             moved = mul(pick[f * face : (f + 1) * face, :], pieces[...])
-            face_send[it, f] = moved[:, 0:cases] + moved[:, cases:]
+            face_send[f] = moved[:, 0:cases] + moved[:, cases:]
 
     def flag(f):
         return adj_ref[0, f].astype(F32)
@@ -249,10 +331,11 @@
             )
             free = 1.0 - glued
             row_weight[i * step : (i + 1) * step, :] = 0.5 + 0.5 * free
-            row_clamp[i * step : (i + 1) * step, :] = touching * free
+            floor = jnp.where(touching * free > 0.5, 0.0, LOWEST)
+            row_floor[i * step : (i + 1) * step, :] = wide(floor)
 
     def clamped(at, value):
-        return jnp.where(wide(row_clamp[at, :]) > 0.5, jnp.maximum(value, 0.0), value)
+        return jnp.maximum(value, row_floor[at, :])
 
     def all_sum(it, totals):
         parts = cases // LANES
@@ -267,8 +350,8 @@
             return pltpu.make_async_remote_copy(
                 src_ref=first_send.at[it],
                 dst_ref=first_recv.at[it, k],
-                send_sem=first_sems.at[it, 0, k],
-                recv_sem=first_sems.at[it, 1, k],
+                send_sem=first_sems.at[0, k],
+                recv_sem=first_sems.at[1, k],
                 device_id=(row, lax.rem(col + k, cols)),
                 device_id_type=MESH,
             )
@@ -284,8 +367,8 @@
             return pltpu.make_async_remote_copy(
                 src_ref=second_send.at[it],
                 dst_ref=second_recv.at[it, k],
-                send_sem=second_sems.at[it, 0, k],
-                recv_sem=second_sems.at[it, 1, k],
+                send_sem=second_sems.at[0, k],
+                recv_sem=second_sems.at[1, k],
                 device_id=(lax.rem(row + k, rows), col),
                 device_id_type=MESH,
             )
@@ -305,16 +388,28 @@
 
     for it in range(ITERS):
         if it == 0:
+            fill_pick((0, 1))
+            loads_copy.wait()
             each_block(negate)
-            faces_of_field(it)
+            faces_of_field(it, (0, 1))
+            greet()
+            tick(it, "faces")
+            fill_pick((2, 3))
+            send_modes()
+            faces_of_field(it, (2, 3))
+            for f in (2, 3):
+                start_side(f, face_send.at[f], face_recv, face_sems)
+            tick(it, "sides")
+            fill_place()
             for f in range(4):
                 wait_side(f, mode_recv, mode_sems)
             for f in range(4):
                 mode_recv[f] = mode_recv[f] * flag(f)
             for f in range(4):
-                product_send[it, f] = mul_split(halves(mode_recv[f]), halves(face_send[it, f]))
+                product_send[it, f] = mul_split(halves(mode_recv[f]), halves(face_send[f]))
             for f in range(4):
-                start_side(f, product_send.at[it, f], product_recv.at[it], product_sems.at[it])
+                start_side(f, product_send.at[it, f], product_recv.at[it], product_sems)
+            tick(it, "products")
             own = mul_split(
                 (modes_high[0:mode_count], modes_low[0:mode_count]),
                 (pieces[:, 0:cases], pieces[:, cases:]),
@@ -327,10 +422,14 @@
             for f in range(4):
                 product_send[it, f] = products[(f + 1) * mode_count : (f + 2) * mode_count]
             for f in range(4):
-                start_side(f, product_send.at[it, f], product_recv.at[it], product_sems.at[it])
-            faces_of_field(it)
+                start_side(f, product_send.at[it, f], product_recv.at[it], product_sems)
+            tick(it, "products")
+            faces_of_field(it, (2, 3))
+            for f in (2, 3):
+                start_side(f, face_send.at[f], face_recv, face_sems)
+            tick(it, "sides")
         for f in range(4):
-            wait_side(f, product_recv.at[it], product_sems.at[it])
+            wait_side(f, product_recv.at[it], product_sems)
             own = own + product_recv[it, f]
         coef_send[it] = own
 
@@ -338,8 +437,8 @@
             return pltpu.make_async_remote_copy(
                 src_ref=coef_send.at[it],
                 dst_ref=coef_recv.at[it, coef_slot],
-                send_sem=coef_sems.at[it, 0, k],
-                recv_sem=coef_sems.at[it, 1, coef_slot],
+                send_sem=coef_sems.at[0, k],
+                recv_sem=coef_sems.at[1, coef_slot],
                 device_id=(lax.rem(row + k, rows), coef_col),
                 device_id_type=MESH,
             )
@@ -357,11 +456,13 @@
 
             else:
                 coef(k).start()
-        for f in range(4):
-            start_side(f, face_send.at[it, f], face_recv.at[it], face_sems.at[it])
+        tick(it, "coefs")
         if it == 0:
             fill_modes()
             fill_rows()
+            op_copy.wait()
+            pick_op(0)
+            tile_copy.wait()
         for k in range(group):
             is_me = (source_row == row) & (source_col + k == col)
 
@@ -370,50 +471,89 @@
                 pltpu.make_async_remote_copy(
                     src_ref=coef_send.at[it],
                     dst_ref=coef_recv.at[it, k],
-                    send_sem=coef_sems.at[it, 0, 0],
-                    recv_sem=coef_sems.at[it, 1, k],
+                    send_sem=coef_sems.at[0, 0],
+                    recv_sem=coef_sems.at[1, k],
                     device_id=(source_row, source_col + k),
                     device_id_type=MESH,
                 ).wait_recv()
 
         block = coef_recv[it].reshape(group * mode_count, cases)
-        part_send[it] = mul_split(halves(tile_ref[...]), halves(block)).reshape(
-            cols, mode_count, cases
-        )
+        partial = mul_split(halves(tile_ref[...]), halves(block)).reshape(
+            cols // 2, 2, mode_count, cases
+        )
+        part_send[it, 0] = partial[:, 0]
+        part_send[it, 1] = partial[:, 1]
+        core = lax.rem(col, 2)
+        pair = pltpu.make_async_remote_copy(
+            src_ref=part_send.at[it, 1 - core],
+            dst_ref=pair_recv.at[it],
+            send_sem=pair_sems.at[0],
+            recv_sem=pair_sems.at[1],
+            device_id=(row, col + 1 - 2 * core),
+            device_id_type=MESH,
+        )
+        pair.start()
+        pair.wait_recv()
+        pair_send[it] = part_send[it, core] + pair_recv[it]
 
         def part(k):
-            target = lax.rem(col + k, cols)
+            target = lax.rem(col + 2 * k, cols)
             return pltpu.make_async_remote_copy(
-                src_ref=part_send.at[it, target],
+                src_ref=pair_send.at[it, target // 2],
                 dst_ref=part_recv.at[it, k],
-                send_sem=part_sems.at[it, 0, k],
-                recv_sem=part_sems.at[it, 1, k],
+                send_sem=part_sems.at[0, k],
+                recv_sem=part_sems.at[1, k],
                 device_id=(row, target),
                 device_id_type=MESH,
             )
 
-        for k in range(1, cols):
+        for k in range(1, cols // 2):
             part(k).start()
-        for k in range(1, cols):
+        def spread(f, at):
+            high, low = halves(face_recv[f, at] * flag(f))
+            return jnp.concatenate([high, low], axis=1)
+
+        def add_sides():
+            for f in (2, 3):
+                pieces[f * face : (f + 1) * face, :] = spread(f, slice(0, face))
+
+            def add(at):
+                moved = mul(place[at, 2 * face : 4 * face], pieces[2 * face : 4 * face, :])
+                field[at, :] = field[at, :] + (moved[:, 0:cases] + moved[:, cases:])
+
+            each_block(add)
+
+        def add_strips(j):
+            tall = 2 * (face // TICKS)
+            span = slice(j // 2 * tall, (j // 2 + 1) * tall)
+            lower = slice(face + j // 2 * tall, face + (j // 2 + 1) * tall)
+            wait_strips(it, j, j + 1)
+            both = jnp.concatenate([spread(0, span), spread(1, span)], axis=0)
+
+            def add(at):
+                there = jnp.concatenate([place[at, span], place[at, lower]], axis=1)
+                moved = mul(there, both)
+                field[at, :] = field[at, :] + (moved[:, 0:cases] + moved[:, cases:])
+
+            each_block(add)
+
+        tick(it, "parts")
+        for f in (2, 3):
+            wait_side(f, face_recv, face_sems)
+        add_sides()
+        for k in range(1, cols // 2):
             part(k).wait_recv()
-        amount = part_send[it, col] + part_recv[it, 1:cols].sum(axis=0)
+        amount = pair_send[it, col // 2] + part_recv[it, 1 : cols // 2].sum(axis=0)
         amount_send[it] = amount
         for f in range(4):
-            start_side(f, amount_send.at[it], amount_recv.at[it], amount_sems.at[it])
-
+            start_side(f, amount_send.at[it], amount_recv.at[it], amount_sems)
+        tick(it, "amounts")
+        if it == 0:
+            pick_op(1)
+        for j in range(0, TICKS, 2):
+            add_strips(j)
         for f in range(4):
-            wait_side(f, face_recv.at[it], face_sems.at[it])
-            high, low = halves(face_recv[it, f] * flag(f))
-            pieces[f * face : (f + 1) * face, 0:cases] = high
-            pieces[f * face : (f + 1) * face, cases:] = low
-
-        def add_faces(at):
-            moved = mul(place[at, :], pieces[...])
-            field[at, :] = field[at, :] + (moved[:, 0:cases] + moved[:, cases:])
-
-        each_block(add_faces)
-        for f in range(4):
-            wait_side(f, amount_recv.at[it], amount_sems.at[it])
+            wait_side(f, amount_recv.at[it], amount_sems)
         amounts = halves(
             jnp.concatenate([amount] + [amount_recv[it, f] for f in range(4)], axis=0)
         )
@@ -426,9 +566,6 @@
             return total + by_eight(wide(row_weight[at, :]) * value * value)
 
         top = lax.fori_loop(0, blocks, turn, jnp.zeros((8, cases), F32))
-        if it == 0:
-            op_copy.wait()
-
         def operate(i, total):
             at = pl.ds(pl.multiple_of(i * step, step), step)
             return total + by_eight(direction[at, :] * mul(op_ref[at, :], direction_half[...]))
@@ -437,16 +574,41 @@
         totals = jnp.concatenate(
             [top.sum(axis=0, keepdims=True), low.sum(axis=0, keepdims=True)], axis=0
         )
+        for f in range(4):
+            if it == 0:
+                sent_side(f, mode_send.at[f], mode_recv, mode_sems)
+            sent_side(f, product_send.at[it, f], product_recv.at[it], product_sems)
+            if f >= 2:
+                sent_side(f, face_send.at[f], face_recv, face_sems)
+            sent_side(f, amount_send.at[it], amount_recv.at[it], amount_sems)
+        for k in range(rows):
+            if k == 0:
+
+                @pl.when(jnp.logical_not(at_home))
+                def _():
+                    coef(0).wait_send()
+
+            else:
+                coef(k).wait_send()
+        for k in range(1, cols // 2):
+            part(k).wait_send()
+        pair.wait_send()
+        sent_strips(it)
         length = all_sum(it, totals)
 
         if it == 0:
 
             def first_update(at):
                 value = clamped(at, 0.0 - length * direction[at, :])
-                out_ref[at, :] = value
+                first_value[at, :] = value
                 direction_half[at, :] = value.astype(BF16)
 
             each_block(first_update)
+            for f in (0, 1):
+                face_send[f] = face_send[f] + mul(
+                    face_op[f * face : (f + 1) * face, :], direction_half[...]
+                )
+            tick(it + 1, "faces")
 
             def local_term(at):
                 value = mul(op_ref[at, :], direction_half[...]) - loads_ref[at, :]
@@ -458,28 +620,17 @@
             each_block(local_term)
         else:
 
-            def last_update(at):
-                out_ref[at, :] = clamped(at, out_ref[at, :] - length * direction[at, :])
-
-            each_block(last_update)
-
-        for f in range(4):
-            if it == 0:
-                sent_side(f, mode_send.at[f], mode_recv, mode_sems)
-            sent_side(f, product_send.at[it, f], product_recv.at[it], product_sems.at[it])
-            sent_side(f, face_send.at[it, f], face_recv.at[it], face_sems.at[it])
-            sent_side(f, amount_send.at[it], amount_recv.at[it], amount_sems.at[it])
-        for k in range(rows):
-            if k == 0:
-
-                @pl.when(jnp.logical_not(at_home))
-                def _():
-                    coef(0).wait_send()
-
-            else:
-                coef(k).wait_send()
-        for k in range(1, cols):
-            part(k).wait_send()
+            def out_copy(i):
+                at = slice(i * step, (i + 1) * step)
+                return pltpu.make_async_copy(field.at[at], out_hbm.at[at], local_sems.at[3 + i])
+
+            for i in range(blocks):
+                at = slice(i * step, (i + 1) * step)
+                field[at, :] = clamped(at, first_value[at, :] - length * direction[at, :])
+                out_copy(i).start()
+
+    for i in range(blocks):
+        out_copy(i).wait()
 
 
 def per_device(rows, cols, local_ops, loads, modes, coarse_inverse, face_rows, adjacency, contact):
@@ -491,52 +642,61 @@
     vmem = pl.BlockSpec(memory_space=pltpu.VMEM)
     dma = pltpu.SemaphoreType.DMA
     scratch = [
+        pltpu.VMEM((order, cases), F32),
+        pltpu.VMEM(coarse_inverse.shape, F32),
         pltpu.VMEM((order, order), BF16),
         pltpu.VMEM((order, order), BF16),
         pltpu.VMEM((order, order), BF16),
+        pltpu.VMEM((2 * face, order), BF16),
         pltpu.VMEM((order, 2 * cases), BF16),
         pltpu.VMEM((stack, order), BF16),
         pltpu.VMEM((stack, order), BF16),
         pltpu.VMEM((order, stack), BF16),
         pltpu.VMEM((order, stack), BF16),
         pltpu.VMEM((order, LANES), F32),
-        pltpu.VMEM((order, LANES), F32),
+        pltpu.VMEM((order, cases), F32),
+        pltpu.VMEM((order, cases), F32),
         pltpu.VMEM((order, cases), F32),
         pltpu.VMEM((order, cases), F32),
         pltpu.VMEM((order, cases), BF16),
         pltpu.VMEM((4, mode_count, face), F32),
         pltpu.VMEM((4, mode_count, face), F32),
-        pltpu.VMEM((ITERS, 4, face, cases), F32),
-        pltpu.VMEM((ITERS, 4, face, cases), F32),
+        pltpu.VMEM((4, face, cases), F32),
+        pltpu.VMEM((4, face, cases), F32),
         pltpu.VMEM((ITERS, 4, mode_count, cases), F32),
         pltpu.VMEM((ITERS, 4, mode_count, cases), F32),
         pltpu.VMEM((ITERS, mode_count, cases), F32),
         pltpu.VMEM((ITERS, group, mode_count, cases), F32),
-        pltpu.VMEM((ITERS, cols, mode_count, cases), F32),
-        pltpu.VMEM((ITERS, cols, mode_count, cases), F32),
+        pltpu.VMEM((ITERS, 2, cols // 2, mode_count, cases), F32),
+        pltpu.VMEM((ITERS, cols // 2, mode_count, cases), F32),
+        pltpu.VMEM((ITERS, cols // 2, mode_count, cases), F32),
+        pltpu.VMEM((ITERS, cols // 2, mode_count, cases), F32),
         pltpu.VMEM((ITERS, mode_count, cases), F32),
         pltpu.VMEM((ITERS, 4, mode_count, cases), F32),
         pltpu.VMEM((ITERS, 8, LANES), F32),
         pltpu.VMEM((ITERS, cols, 8, LANES), F32),
         pltpu.VMEM((ITERS, 8, LANES), F32),
         pltpu.VMEM((ITERS, rows, 8, LANES), F32),
-        dma,
+        dma((3 + 4,)),
         dma((2, 4)),
-        dma((ITERS, 2, 4)),
-        dma((ITERS, 2, 4)),
-        dma((ITERS, 2, max(rows, group))),
-        dma((ITERS, 2, cols)),
-        dma((ITERS, 2, 4)),
-        dma((ITERS, 2, cols)),
-        dma((ITERS, 2, rows)),
+        dma((2, 4)),
+        dma((2, 2, TICKS)),
+        dma((2, 4)),
+        dma((2, max(rows, group))),
+        dma((2,)),
+        dma((2, cols // 2)),
+        dma((2, 4)),
+        dma((2, cols)),
+        dma((2, rows)),
     ]
+    anywhere = pl.BlockSpec(memory_space=pl.ANY)
     result = pl.pallas_call(
         functools.partial(kernel, rows, cols),
         out_shape=jax.ShapeDtypeStruct((order, cases), F32),
         in_specs=[pl.BlockSpec(memory_space=pltpu.SMEM)]
-        + [vmem] * 5
-        + [pl.BlockSpec(memory_space=pl.ANY)],
-        out_specs=vmem,
+        + [vmem] * 3
+        + [anywhere] * 3,
+        out_specs=anywhere,
         scratch_shapes=scratch,
         compiler_params=pltpu.CompilerParams(
             collective_id=0, has_side_effects=True, vmem_limit_bytes=VMEM_BYTES
@@ -545,10 +705,10 @@
     )(
         adjacency[0],
         modes[0, 0],
+        face_rows[0, 0],
+        contact[0],
         loads[0, 0],
         coarse_inverse,
-        face_rows[0, 0],
-        contact[0],
         local_ops[0, 0],
     )
     return result[None, None]

time: 157 us -> 139 us (0.89)
  Pallas kernels: 154 us -> 136 us
    pallas_call x1, Pallas kernels: 154 us -> 136 us  [per_device(): pl.pallas_call(functools.partial(kernel, rows, cols), out_shape=jax.Shape...]
where the time goes in v2:
time: 139 us
  Pallas kernels  136 us (98%)
  local copies, waits for them, and re-layouts  3.05 us (2%)
    pallas_call x1, Pallas kernels, per_device(): pl.pallas_call(functools.partial(kernel, rows, cols), out_shape=jax.Shape...  136 us
    unnamed x1, local copies, waits for them, and re-layouts  3.05 us

profile of v2, /device:TPU:1, one launch (start us, length us, event | category | flops | bytes accessed | tf_op | source)
XLA Modules:
  0.0 139.0 jit_solution(7695307471276282495)
XLA Ops:
  0.0 135.9 %dual_steps.1 = f32[2048,256]{1,0:T(8,128)} custom-call(s32[1,4]{1,0:T(1,128)} %bitcast.13, f32[32,2048]{1,0:T(8,128)} %bitcast.10, s32[4,512]{1,0:T(4,128)} %bitcast.11, s32[1,2048]{1,0:T(1,128)} %bitcast.12, f32[2048,256]{1,0:T(8,128)} %bitcast.9, f32[512,256]{1,0:T(8,128)} %tile_hbm.1, bf16[2048,2048]{1,0:T(8,128)(2,1)} %bitcast.7), custom_call_target="tpu_custom_call" | custom-call | tf_op jit(solution)/shard_map/dual_steps/pallas_call | solution.py:693
  135.9 3.0 %copy.9 = f32[1,1,2048,256]{3,2,1,0:T(8,128)} copy(f32[1,1,2048,256]{3,2,1,0:T(8,128)} %bitcast.8) | data formatting | bytes 4194304

commit v3 on v2

--- a/solution.py
+++ b/solution.py
@@ -15,10 +15,12 @@
 VMEM_BYTES = 63_000_000
 TICKS = 8
 SCHEDULE = (
-    {"faces": (0, 1), "sides": (2,), "products": (3,), "coefs": (4, 5), "parts": (6, 7)},
-    {"faces": (0, 1), "coefs": (2, 3), "parts": (4, 5, 6, 7)},
+    {"faces": (0,), "products": (1,), "coefs": (2, 3, 4), "parts": (5, 6), "amounts": (7,)},
+    {"faces": (0, 1), "parts": (2, 3, 4), "amounts": (5, 6, 7)},
 )
+AHEAD = 2
 LOWEST = float(jnp.finfo(jnp.float32).min)
+EARLY = (4, 0)
 
 
 def halves(value):
@@ -62,6 +64,9 @@
     pick,
     place,
     face_op,
+    mode_op_high,
+    mode_op_low,
+    first_own,
     pieces,
     modes_high,
     modes_low,
@@ -77,6 +82,7 @@
     mode_recv,
     face_send,
     face_recv,
+    passing,
     product_send,
     product_recv,
     coef_send,
@@ -94,6 +100,7 @@
     local_sems,
     mode_sems,
     face_sems,
+    pass_sems,
     strip_sems,
     product_sems,
     coef_sems,
@@ -111,6 +118,7 @@
     group = coef_recv.shape[1]
     step = 512
     blocks = order // step
+    ahead = AHEAD * (face // TICKS)
 
     loads_copy = pltpu.make_async_copy(loads_hbm, loads_ref, local_sems.at[0])
     tile_copy = pltpu.make_async_copy(tile_hbm, tile_ref, local_sems.at[1])
@@ -203,7 +211,7 @@
                     BF16
                 )
 
-    def send_modes():
+    def make_modes():
         high, low = halves(modes_ref[...])
         modes_high[0:mode_count] = high
         modes_low[0:mode_count] = low
@@ -216,21 +224,31 @@
                 preferred_element_type=F32,
             )
             mode_send[f] = moved[0:mode_count] + moved[mode_count:]
-        for f in range(4):
-            start_side(f, mode_send.at[f], mode_recv, mode_sems)
 
     def greet():
         here = (source_row == row) & (source_col <= col) & (col < source_col + group)
         greeted = cols - 1 + rows - 1 + group - here.astype(jnp.int32)
         pl.semaphore_wait(barrier, greeted)
 
-    def pick_op(f):
+    def modes_op():
+        both = jnp.concatenate([modes_high[...], modes_low[...]], axis=0)
+        count = modes_high.shape[0]
+
         @pl.loop(0, order // step)
         def _(i):
             at = pl.ds(pl.multiple_of(i * step, step), step)
-            face_op[f * face : (f + 1) * face, at] = mul(
-                pick[f * face : (f + 1) * face, :], op_ref[:, at]
-            ).astype(BF16)
+            moved = mul(both, op_ref[:, at])
+            high, low = halves(moved[0:count] + moved[count:])
+            mode_op_high[:, at] = high
+            mode_op_low[:, at] = low
+
+    def pick_op():
+        both = jnp.concatenate([pick[0:ahead, :], pick[face : face + ahead, :]], axis=0)
+
+        @pl.loop(0, order // step)
+        def _(i):
+            at = pl.ds(pl.multiple_of(i * step, step), step)
+            face_op[:, at] = mul(both, op_ref[:, at]).astype(BF16)
 
     def fill_place():
         @pl.loop(0, order // 256)
@@ -240,6 +258,81 @@
                 here = lax.broadcasted_iota(jnp.int32, (256, face), 0) + i * 256
                 hit = here == index_ref[f : f + 1, :]
                 place[at, f * face : (f + 1) * face] = jnp.where(hit, 1.0, 0.0).astype(BF16)
+
+    seam = cols // 2
+    crossing = {2: col == seam, 3: col == seam - 1}
+    over = {2: 1, 3: cols - 2}
+    short = face // 2
+
+    def lateral(f, part, incoming):
+        at = pl.ds(part * short, short)
+        return pltpu.make_async_remote_copy(
+            src_ref=face_recv.at[f, at] if incoming else face_send.at[f, at],
+            dst_ref=face_recv.at[f if incoming else f ^ 1, at],
+            send_sem=face_sems.at[0, f, part],
+            recv_sem=face_sems.at[1, f if incoming else f ^ 1, part],
+            device_id=sides[f][1],
+            device_id_type=MESH,
+        )
+
+    def detour(f):
+        return pltpu.make_async_remote_copy(
+            src_ref=face_send.at[f, pl.ds(short, short)],
+            dst_ref=passing,
+            send_sem=face_sems.at[0, f, 1],
+            recv_sem=pass_sems.at[0],
+            device_id=(row, over[f]),
+            device_id_type=MESH,
+        )
+
+    def onward(f):
+        return pltpu.make_async_remote_copy(
+            src_ref=passing,
+            dst_ref=face_recv.at[f ^ 1, pl.ds(short, short)],
+            send_sem=pass_sems.at[1],
+            recv_sem=face_sems.at[1, f ^ 1, 1],
+            device_id=(row, seam - 1 if f == 2 else seam),
+            device_id_type=MESH,
+        )
+
+    def start_lateral(f):
+        @pl.when(sides[f][0])
+        def _():
+            lateral(f, 0, False).start()
+
+        @pl.when(sides[f][0] & jnp.logical_not(crossing[f]))
+        def _():
+            lateral(f, 1, False).start()
+
+        @pl.when(crossing[f])
+        def _():
+            detour(f).start()
+
+    def pass_lateral():
+        for f in (2, 3):
+
+            @pl.when(col == over[f])
+            def _():
+                detour(f).wait_recv()
+                onward(f).start()
+
+    def wait_lateral(f):
+        for part in range(2):
+
+            @pl.when(sides[f][0])
+            def _():
+                lateral(f, part, True).wait_recv()
+
+    def sent_lateral(f):
+        for part in range(2):
+
+            @pl.when(sides[f][0])
+            def _():
+                lateral(f, part, False).wait_send()
+
+        @pl.when(col == over[f])
+        def _():
+            onward(f).wait_send()
 
     def strip(it, f, j, incoming):
         tall = face // TICKS
@@ -332,10 +425,10 @@
             free = 1.0 - glued
             row_weight[i * step : (i + 1) * step, :] = 0.5 + 0.5 * free
             floor = jnp.where(touching * free > 0.5, 0.0, LOWEST)
-            row_floor[i * step : (i + 1) * step, :] = wide(floor)
+            row_floor[i * step : (i + 1) * step, :] = floor
 
     def clamped(at, value):
-        return jnp.maximum(value, row_floor[at, :])
+        return jnp.maximum(value, wide(row_floor[at, :]))
 
     def all_sum(it, totals):
         parts = cases // LANES
@@ -388,19 +481,16 @@
 
     for it in range(ITERS):
         if it == 0:
-            fill_pick((0, 1))
+            fill_pick((0, 1, 2, 3))
+            make_modes()
+            greet()
+            for f in range(4):
+                start_side(f, mode_send.at[f], mode_recv, mode_sems)
             loads_copy.wait()
             each_block(negate)
             faces_of_field(it, (0, 1))
-            greet()
             tick(it, "faces")
-            fill_pick((2, 3))
-            send_modes()
             faces_of_field(it, (2, 3))
-            for f in (2, 3):
-                start_side(f, face_send.at[f], face_recv, face_sems)
-            tick(it, "sides")
-            fill_place()
             for f in range(4):
                 wait_side(f, mode_recv, mode_sems)
             for f in range(4):
@@ -410,24 +500,16 @@
             for f in range(4):
                 start_side(f, product_send.at[it, f], product_recv.at[it], product_sems)
             tick(it, "products")
+            for f in (2, 3):
+                start_lateral(f)
+            fill_place()
             own = mul_split(
                 (modes_high[0:mode_count], modes_low[0:mode_count]),
                 (pieces[:, 0:cases], pieces[:, cases:]),
             )
+            first_own[...] = own
         else:
-            products = mul_split(
-                (modes_high[...], modes_low[...]), (pieces[:, 0:cases], pieces[:, cases:])
-            )
-            own = products[0:mode_count]
-            for f in range(4):
-                product_send[it, f] = products[(f + 1) * mode_count : (f + 2) * mode_count]
-            for f in range(4):
-                start_side(f, product_send.at[it, f], product_recv.at[it], product_sems)
-            tick(it, "products")
-            faces_of_field(it, (2, 3))
-            for f in (2, 3):
-                start_side(f, face_send.at[f], face_recv, face_sems)
-            tick(it, "sides")
+            own = next_own
         for f in range(4):
             wait_side(f, product_recv.at[it], product_sems)
             own = own + product_recv[it, f]
@@ -457,11 +539,16 @@
             else:
                 coef(k).start()
         tick(it, "coefs")
+        if it == 1:
+            faces_of_field(it, (2, 3))
+            for f in (2, 3):
+                start_lateral(f)
         if it == 0:
             fill_modes()
             fill_rows()
             op_copy.wait()
-            pick_op(0)
+            pick_op()
+            modes_op()
             tile_copy.wait()
         for k in range(group):
             is_me = (source_row == row) & (source_col + k == col)
@@ -523,12 +610,15 @@
 
             each_block(add)
 
-        def add_strips(j):
+        def strips(j):
             tall = 2 * (face // TICKS)
             span = slice(j // 2 * tall, (j // 2 + 1) * tall)
             lower = slice(face + j // 2 * tall, face + (j // 2 + 1) * tall)
             wait_strips(it, j, j + 1)
-            both = jnp.concatenate([spread(0, span), spread(1, span)], axis=0)
+            return span, lower, jnp.concatenate([spread(0, span), spread(1, span)], axis=0)
+
+        def add_strips(j):
+            span, lower, both = strips(j)
 
             def add(at):
                 there = jnp.concatenate([place[at, span], place[at, lower]], axis=1)
@@ -538,9 +628,9 @@
             each_block(add)
 
         tick(it, "parts")
-        for f in (2, 3):
-            wait_side(f, face_recv, face_sems)
-        add_sides()
+        pass_lateral()
+        for j in range(0, EARLY[it], 2):
+            add_strips(j)
         for k in range(1, cols // 2):
             part(k).wait_recv()
         amount = pair_send[it, col // 2] + part_recv[it, 1 : cols // 2].sum(axis=0)
@@ -548,9 +638,10 @@
         for f in range(4):
             start_side(f, amount_send.at[it], amount_recv.at[it], amount_sems)
         tick(it, "amounts")
-        if it == 0:
-            pick_op(1)
-        for j in range(0, TICKS, 2):
+        for f in (2, 3):
+            wait_lateral(f)
+        add_sides()
+        for j in range(EARLY[it], TICKS - 2, 2):
             add_strips(j)
         for f in range(4):
             wait_side(f, amount_recv.at[it], amount_sems)
@@ -558,9 +649,19 @@
             jnp.concatenate([amount] + [amount_recv[it, f] for f in range(4)], axis=0)
         )
 
+        def correct(at):
+            field[at, :] = field[at, :] - mul_split(
+                (modes_high_t[at, :], modes_low_t[at, :]), amounts
+            )
+
+        each_block(correct)
+        last, lower, both = strips(TICKS - 2)
+
         def turn(i, total):
             at = pl.ds(pl.multiple_of(i * step, step), step)
-            value = field[at, :] - mul_split((modes_high_t[at, :], modes_low_t[at, :]), amounts)
+            there = jnp.concatenate([place[at, last], place[at, lower]], axis=1)
+            moved = mul(there, both)
+            value = field[at, :] + (moved[:, 0:cases] + moved[:, cases:])
             direction[at, :] = value
             direction_half[at, :] = value.astype(BF16)
             return total + by_eight(wide(row_weight[at, :]) * value * value)
@@ -579,7 +680,7 @@
                 sent_side(f, mode_send.at[f], mode_recv, mode_sems)
             sent_side(f, product_send.at[it, f], product_recv.at[it], product_sems)
             if f >= 2:
-                sent_side(f, face_send.at[f], face_recv, face_sems)
+                sent_lateral(f)
             sent_side(f, amount_send.at[it], amount_recv.at[it], amount_sems)
         for k in range(rows):
             if k == 0:
@@ -604,10 +705,18 @@
                 direction_half[at, :] = value.astype(BF16)
 
             each_block(first_update)
+            products = mul(mode_op_high[...], direction_half[...]) + mul(
+                mode_op_low[...], direction_half[...]
+            )
+            next_own = products[0:mode_count] + first_own[...]
+            for f in range(4):
+                at = slice((f + 1) * mode_count, (f + 2) * mode_count)
+                product_send[it + 1, f] = products[at] + product_send[it, f]
+            for f in range(4):
+                start_side(f, product_send.at[it + 1, f], product_recv.at[it + 1], product_sems)
+            moved = mul(face_op[...], direction_half[...])
             for f in (0, 1):
-                face_send[f] = face_send[f] + mul(
-                    face_op[f * face : (f + 1) * face, :], direction_half[...]
-                )
+                face_send[f, 0:ahead] = face_send[f, 0:ahead] + moved[f * ahead : (f + 1) * ahead]
             tick(it + 1, "faces")
 
             def local_term(at):
@@ -618,6 +727,10 @@
                 pieces[at, cases:] = low
 
             each_block(local_term)
+            for f in (0, 1):
+                moved = mul(pick[f * face + ahead : (f + 1) * face, :], pieces[...])
+                face_send[f, ahead:] = moved[:, 0:cases] + moved[:, cases:]
+            tick(it + 1, "sides")
         else:
 
             def out_copy(i):
@@ -647,14 +760,17 @@
         pltpu.VMEM((order, order), BF16),
         pltpu.VMEM((order, order), BF16),
         pltpu.VMEM((order, order), BF16),
-        pltpu.VMEM((2 * face, order), BF16),
+        pltpu.VMEM((2 * AHEAD * (face // TICKS), order), BF16),
+        pltpu.VMEM((stack, order), BF16),
+        pltpu.VMEM((stack, order), BF16),
+        pltpu.VMEM((mode_count, cases), F32),
         pltpu.VMEM((order, 2 * cases), BF16),
         pltpu.VMEM((stack, order), BF16),
         pltpu.VMEM((stack, order), BF16),
         pltpu.VMEM((order, stack), BF16),
         pltpu.VMEM((order, stack), BF16),
         pltpu.VMEM((order, LANES), F32),
-        pltpu.VMEM((order, cases), F32),
+        pltpu.VMEM((order, LANES), F32),
         pltpu.VMEM((order, cases), F32),
         pltpu.VMEM((order, cases), F32),
         pltpu.VMEM((order, cases), F32),
@@ -663,6 +779,7 @@
         pltpu.VMEM((4, mode_count, face), F32),
         pltpu.VMEM((4, face, cases), F32),
         pltpu.VMEM((4, face, cases), F32),
+        pltpu.VMEM((face // 2, cases), F32),
         pltpu.VMEM((ITERS, 4, mode_count, cases), F32),
         pltpu.VMEM((ITERS, 4, mode_count, cases), F32),
         pltpu.VMEM((ITERS, mode_count, cases), F32),
@@ -679,7 +796,8 @@
         pltpu.VMEM((ITERS, rows, 8, LANES), F32),
         dma((3 + 4,)),
         dma((2, 4)),
-        dma((2, 4)),
+        dma((2, 4, 2)),
+        dma((2,)),
         dma((2, 2, TICKS)),
         dma((2, 4)),
         dma((2, max(rows, group))),

time: 139 us -> 129 us (0.928)
  Pallas kernels: 136 us -> 126 us
    pallas_call x1, Pallas kernels: 136 us -> 126 us  [per_device(): pl.pallas_call(functools.partial(kernel, rows, cols), out_shape=jax.Shape...]
where the time goes in v3:
time: 129 us
  Pallas kernels  126 us (98%)
  local copies, waits for them, and re-layouts  3.05 us (2%)
    pallas_call x1, Pallas kernels, per_device(): pl.pallas_call(functools.partial(kernel, rows, cols), out_shape=jax.Shape...  126 us
    unnamed x1, local copies, waits for them, and re-layouts  3.05 us

profile of v3, /device:TPU:1, one launch (start us, length us, event | category | flops | bytes accessed | tf_op | source)
XLA Modules:
  0.0 129.1 jit_solution(13997012219734325998)
XLA Ops:
  0.0 126.0 %dual_steps.1 = f32[2048,256]{1,0:T(8,128)} custom-call(s32[1,4]{1,0:T(1,128)} %bitcast.13, f32[32,2048]{1,0:T(8,128)} %bitcast.10, s32[4,512]{1,0:T(4,128)} %bitcast.11, s32[1,2048]{1,0:T(1,128)} %bitcast.12, f32[2048,256]{1,0:T(8,128)} %bitcast.9, f32[512,256]{1,0:T(8,128)} %tile_hbm.1, bf16[2048,2048]{1,0:T(8,128)(2,1)} %bitcast.7), custom_call_target="tpu_custom_call" | custom-call | tf_op jit(solution)/shard_map/dual_steps/pallas_call | solution.py:811
  126.0 3.0 %copy.9 = f32[1,1,2048,256]{3,2,1,0:T(8,128)} copy(f32[1,1,2048,256]{3,2,1,0:T(8,128)} %bitcast.8) | data formatting | bytes 4194304

commit v4 on v3

--- a/solution.py
+++ b/solution.py
@@ -15,8 +15,8 @@
 VMEM_BYTES = 63_000_000
 TICKS = 8
 SCHEDULE = (
-    {"faces": (0,), "products": (1,), "coefs": (2, 3, 4), "parts": (5, 6), "amounts": (7,)},
-    {"faces": (0, 1), "parts": (2, 3, 4), "amounts": (5, 6, 7)},
+    {"faces": (0,), "products": (1,), "coefs": (2, 3), "parts": (4, 5, 6), "amounts": (7,)},
+    {"faces": (0, 1), "fill": (2,), "parts": (3, 4, 5), "amounts": (6, 7)},
 )
 AHEAD = 2
 LOWEST = float(jnp.finfo(jnp.float32).min)
@@ -262,6 +262,7 @@
     seam = cols // 2
     crossing = {2: col == seam, 3: col == seam - 1}
     over = {2: 1, 3: cols - 2}
+    around = {2: (1,), 3: (0, 1)}
     short = face // 2
 
     def lateral(f, part, incoming):
@@ -275,46 +276,54 @@
             device_id_type=MESH,
         )
 
-    def detour(f):
+    def detour(f, part):
+        at = pl.ds(part * short, short)
         return pltpu.make_async_remote_copy(
-            src_ref=face_send.at[f, pl.ds(short, short)],
-            dst_ref=passing,
-            send_sem=face_sems.at[0, f, 1],
-            recv_sem=pass_sems.at[0],
+            src_ref=face_send.at[f, at],
+            dst_ref=passing.at[at],
+            send_sem=face_sems.at[0, f, part],
+            recv_sem=pass_sems.at[0, part],
             device_id=(row, over[f]),
             device_id_type=MESH,
         )
 
-    def onward(f):
+    def onward(f, part):
+        at = pl.ds(part * short, short)
         return pltpu.make_async_remote_copy(
-            src_ref=passing,
-            dst_ref=face_recv.at[f ^ 1, pl.ds(short, short)],
-            send_sem=pass_sems.at[1],
-            recv_sem=face_sems.at[1, f ^ 1, 1],
+            src_ref=passing.at[at],
+            dst_ref=face_recv.at[f ^ 1, at],
+            send_sem=pass_sems.at[1, part],
+            recv_sem=face_sems.at[1, f ^ 1, part],
             device_id=(row, seam - 1 if f == 2 else seam),
             device_id_type=MESH,
         )
 
     def start_lateral(f):
-        @pl.when(sides[f][0])
-        def _():
-            lateral(f, 0, False).start()
-
-        @pl.when(sides[f][0] & jnp.logical_not(crossing[f]))
-        def _():
-            lateral(f, 1, False).start()
-
-        @pl.when(crossing[f])
-        def _():
-            detour(f).start()
+        for part in range(2):
+            if part in around[f]:
+
+                @pl.when(sides[f][0] & jnp.logical_not(crossing[f]))
+                def _():
+                    lateral(f, part, False).start()
+
+                @pl.when(crossing[f])
+                def _():
+                    detour(f, part).start()
+
+            else:
+
+                @pl.when(sides[f][0])
+                def _():
+                    lateral(f, part, False).start()
 
     def pass_lateral():
         for f in (2, 3):
 
             @pl.when(col == over[f])
             def _():
-                detour(f).wait_recv()
-                onward(f).start()
+                for part in around[f]:
+                    detour(f, part).wait_recv()
+                    onward(f, part).start()
 
     def wait_lateral(f):
         for part in range(2):
@@ -332,7 +341,8 @@
 
         @pl.when(col == over[f])
         def _():
-            onward(f).wait_send()
+            for part in around[f]:
+                onward(f, part).wait_send()
 
     def strip(it, f, j, incoming):
         tall = face // TICKS
@@ -550,6 +560,7 @@
             pick_op()
             modes_op()
             tile_copy.wait()
+        tick(it, "fill")
         for k in range(group):
             is_me = (source_row == row) & (source_col + k == col)
 
@@ -779,7 +790,7 @@
         pltpu.VMEM((4, mode_count, face), F32),
         pltpu.VMEM((4, face, cases), F32),
         pltpu.VMEM((4, face, cases), F32),
-        pltpu.VMEM((face // 2, cases), F32),
+        pltpu.VMEM((face, cases), F32),
         pltpu.VMEM((ITERS, 4, mode_count, cases), F32),
         pltpu.VMEM((ITERS, 4, mode_count, cases), F32),
         pltpu.VMEM((ITERS, mode_count, cases), F32),
@@ -797,7 +808,7 @@
         dma((3 + 4,)),
         dma((2, 4)),
         dma((2, 4, 2)),
-        dma((2,)),
+        dma((2, 2)),
         dma((2, 2, TICKS)),
         dma((2, 4)),
         dma((2, max(rows, group))),

time: 129 us -> 129 us (level)
  no operation moved by 1% of the time
where the time goes in v4:
time: 129 us
  Pallas kernels  126 us (98%)
  local copies, waits for them, and re-layouts  3.05 us (2%)
    pallas_call x1, Pallas kernels, per_device(): pl.pallas_call(functools.partial(kernel, rows, cols), out_shape=jax.Shape...  126 us
    unnamed x1, local copies, waits for them, and re-layouts  3.05 us

profile of v4, /device:TPU:1, one launch (start us, length us, event | category | flops | bytes accessed | tf_op | source)
XLA Modules:
  0.0 128.8 jit_solution(6008727627741433870)
XLA Ops:
  0.0 125.8 %dual_steps.1 = f32[2048,256]{1,0:T(8,128)} custom-call(s32[1,4]{1,0:T(1,128)} %bitcast.13, f32[32,2048]{1,0:T(8,128)} %bitcast.10, s32[4,512]{1,0:T(4,128)} %bitcast.11, s32[1,2048]{1,0:T(1,128)} %bitcast.12, f32[2048,256]{1,0:T(8,128)} %bitcast.9, f32[512,256]{1,0:T(8,128)} %tile_hbm.1, bf16[2048,2048]{1,0:T(8,128)(2,1)} %bitcast.7), custom_call_target="tpu_custom_call" | custom-call | tf_op jit(solution)/shard_map/dual_steps/pallas_call | solution.py:822
  125.8 3.0 %copy.9 = f32[1,1,2048,256]{3,2,1,0:T(8,128)} copy(f32[1,1,2048,256]{3,2,1,0:T(8,128)} %bitcast.8) | data formatting | bytes 4194304
